TPU v7x, 32 devices: a whole 2x2x4 slice. The times are simulated.
32 devices in a mesh: dp: 8 (over z, x), slot: 4 (over y, core).
Axes of the slice: x: 2, y: 2, z: 4, core: 2. Of those that a mesh axis runs over, the one named last changes fastest.
Arguments:
- byte_ids: int32 [1024, 8], P('dp'), may hold values from 0 to 255
- seg_ids: int32 [8, 128], P('dp'), may hold values from 0 to 1, never falling along the last dimension, each value on 1 to 96 neighbouring positions
- embed_table: bfloat16 [256, 768], P('dp'), may hold values from -6 to 6
- slot_project: bfloat16 [8, 768, 768], P('slot', 'dp'), may hold values from -0.078125 to 0.078125
- patch_prenorm: bfloat16 [768], P('dp'), may hold values from 0.5 to 1.5
- patch_heads: bfloat16 [768, 2304], P('dp'), may hold values from -0.21875 to 0.21875
- patch_mixer: bfloat16 [768, 768], P('dp'), may hold values from -0.875 to 0.875
- patch_midnorm: bfloat16 [768], P('dp'), may hold values from 0.5 to 1.5
- patch_expand: bfloat16 [768, 3072], P('dp'), may hold values from -0.21875 to 0.21875
- patch_reduce: bfloat16 [3072, 768], P('dp'), may hold values from -0.109375 to 0.109375
- byte_prenorm: bfloat16 [768], P('dp'), may hold values from 0.5 to 1.5
- byte_heads: bfloat16 [768, 2304], P('dp'), may hold values from -0.21875 to 0.21875
- byte_mixer: bfloat16 [768, 768], P('dp'), may hold values from -0.4375 to 0.4375
- byte_midnorm: bfloat16 [768], P('dp'), may hold values from 0.5 to 1.5
- byte_expand: bfloat16 [768, 3072], P('dp'), may hold values from -0.21875 to 0.21875
- byte_reduce: bfloat16 [3072, 768], P('dp'), may hold values from -0.109375 to 0.109375
- d_output: bfloat16 [1024, 8, 768], P(('dp', 'slot')), may hold values from -6 to 6
Outputs:
- out_bytes: bfloat16 [1024, 8, 768], P(('dp', 'slot'))
- embed_grad: float32 [256, 768], P('dp')
- project_grad: float32 [8, 768, 768], P('slot', 'dp')
- patch_prenorm_grad: float32 [768], P('dp')
- patch_heads_grad: float32 [768, 2304], P('dp')
- patch_mixer_grad: float32 [768, 768], P('dp')
- patch_midnorm_grad: float32 [768], P('dp')
- patch_expand_grad: float32 [768, 3072], P('dp')
- patch_reduce_grad: float32 [3072, 768], P('dp')
- byte_prenorm_grad: float32 [768], P('dp')
- byte_heads_grad: float32 [768, 2304], P('dp')
- byte_mixer_grad: float32 [768, 768], P('dp')
- byte_midnorm_grad: float32 [768], P('dp')
- byte_expand_grad: float32 [768, 3072], P('dp')
- byte_reduce_grad: float32 [3072, 768], P('dp')
Inputs may be any that keep to these rules, and one draw needn't show every extreme that they name: `seg_ids`: in each row the numbers never fall; each of the 2 sequences covers 1 to 96 patches.
All inputs are finite; a program needn't handle non-finite values.
Results may differ from a plain program's by a relative error of at most 0.03.
Values may be sent and summed in bfloat16 or wider, within the bound.
A program may use at most 192 MiB of HBM per device.

v0:
```python
import math

import jax
import jax.numpy as jnp
from jax import lax
from jax.sharding import PartitionSpec as P

HEAD_DIM = 64


EPSILON = 1e-05
MASKED = -1000000000.0


def norm_rows(values, gain_vec):
    center = jnp.mean(values, axis=-1, keepdims=True)
    shifted = values - center
    spread = jnp.mean(shifted * shifted, axis=-1, keepdims=True)
    return shifted * lax.rsqrt(spread + EPSILON) * gain_vec


def gelu_tanh(values):
    inside = 0.7978845608028654 * (values + 0.044715 * values * values * values)
    return 0.5 * values * (1.0 + jnp.tanh(inside))


def attention(queries, keyset, valueset, allowed):
    scores = jnp.einsum(
        "bnhe,bmhe->bhnm", queries, keyset, preferred_element_type=jnp.float32
    ) * HEAD_DIM ** (-0.5)
    scores = jnp.where(allowed[:, None], scores, MASKED)
    highest = jnp.max(scores, axis=-1, keepdims=True)
    exponents = jnp.exp(scores - highest)
    totals = jnp.sum(exponents, axis=-1, keepdims=True)
    softened = (exponents / totals).astype(jnp.bfloat16)
    mixture = jnp.einsum("bhnm,bmhe->bnhe", softened, valueset, preferred_element_type=jnp.float32)
    return (mixture, highest + jnp.log(totals))


def attention_back(queries, keyset, valueset, allowed, logsum, d_mixture):
    scale_value = HEAD_DIM ** (-0.5)
    scores = (
        jnp.einsum("bnhe,bmhe->bhnm", queries, keyset, preferred_element_type=jnp.float32)
        * scale_value
    )
    scores = jnp.where(allowed[:, None], scores, MASKED)
    softened = jnp.exp(scores - logsum)
    d_soft = jnp.einsum("bnhe,bmhe->bhnm", d_mixture, valueset, preferred_element_type=jnp.float32)
    inside = jnp.sum(d_soft * softened, axis=-1, keepdims=True)
    d_scores = (softened * (d_soft - inside)).astype(jnp.bfloat16)
    d_queries = (
        jnp.einsum("bhnm,bmhe->bnhe", d_scores, keyset, preferred_element_type=jnp.float32)
        * scale_value
    )
    d_keys = (
        jnp.einsum("bhnm,bnhe->bmhe", d_scores, queries, preferred_element_type=jnp.float32)
        * scale_value
    )
    d_values = jnp.einsum(
        "bhnm,bnhe->bmhe",
        softened.astype(jnp.bfloat16),
        d_mixture,
        preferred_element_type=jnp.float32,
    )
    return (d_queries, d_keys, d_values)


def block_forward(values, weights, attend):
    gain_one, w_heads, w_mixer, gain_two, w_expand, w_reduce = weights
    batch, row_count, width = values.shape
    head_count = width // HEAD_DIM
    norm_one, back_one = jax.vjp(norm_rows, values, gain_one.astype(jnp.float32))
    norm_one = norm_one.astype(jnp.bfloat16)
    joined = jnp.einsum(
        "bnd,df->bnf", norm_one, w_heads, preferred_element_type=jnp.float32
    ).astype(jnp.bfloat16)
    joined = joined.reshape(batch, row_count, 3, head_count, HEAD_DIM)
    mixture, kept = attend(joined[:, :, 0], joined[:, :, 1], joined[:, :, 2])
    mixture = mixture.astype(jnp.bfloat16).reshape(batch, row_count, width)
    middle = values + jnp.einsum(
        "bnf,fd->bnd", mixture, w_mixer, preferred_element_type=jnp.float32
    )
    norm_two, back_two = jax.vjp(norm_rows, middle, gain_two.astype(jnp.float32))
    norm_two = norm_two.astype(jnp.bfloat16)
    expanded = jnp.einsum("bnd,df->bnf", norm_two, w_expand, preferred_element_type=jnp.float32)
    hidden, back_gelu = jax.vjp(gelu_tanh, expanded)
    hidden = hidden.astype(jnp.bfloat16)
    result = middle + jnp.einsum(
        "bnf,fd->bnd", hidden, w_reduce, preferred_element_type=jnp.float32
    )
    saved = (back_one, norm_one, joined, kept, mixture, back_two, norm_two, back_gelu, hidden)
    return (result, saved)


def block_backward(grad_out, weights, saved, attend_back):
    gain_one, w_heads, w_mixer, gain_two, w_expand, w_reduce = weights
    back_one, norm_one, joined, kept, mixture, back_two, norm_two, back_gelu, hidden = saved
    batch, row_count, width = grad_out.shape
    grad_low = grad_out.astype(jnp.bfloat16)
    reduce_grad = jnp.einsum("bnf,bnd->fd", hidden, grad_low, preferred_element_type=jnp.float32)
    d_hidden = jnp.einsum("bnd,fd->bnf", grad_low, w_reduce, preferred_element_type=jnp.float32)
    (d_expanded,) = back_gelu(d_hidden)
    d_expanded = d_expanded.astype(jnp.bfloat16)
    expand_grad = jnp.einsum(
        "bnd,bnf->df", norm_two, d_expanded, preferred_element_type=jnp.float32
    )
    d_norm_two = jnp.einsum("bnf,df->bnd", d_expanded, w_expand, preferred_element_type=jnp.float32)
    d_middle_part, midnorm_grad = back_two(d_norm_two)
    d_middle = grad_out + d_middle_part
    middle_low = d_middle.astype(jnp.bfloat16)
    mixer_grad = jnp.einsum("bnf,bnd->fd", mixture, middle_low, preferred_element_type=jnp.float32)
    d_mixture = jnp.einsum(
        "bnd,fd->bnf", middle_low, w_mixer, preferred_element_type=jnp.float32
    ).astype(jnp.bfloat16)
    d_mixture = d_mixture.reshape(batch, row_count, width // HEAD_DIM, HEAD_DIM)
    d_queries, d_keys, d_values = attend_back(
        joined[:, :, 0], joined[:, :, 1], joined[:, :, 2], kept, d_mixture
    )
    d_joined = (
        jnp.stack([d_queries, d_keys, d_values], axis=2)
        .reshape(batch, row_count, 3 * width)
        .astype(jnp.bfloat16)
    )
    heads_grad = jnp.einsum("bnd,bnf->df", norm_one, d_joined, preferred_element_type=jnp.float32)
    d_norm_one = jnp.einsum("bnf,df->bnd", d_joined, w_heads, preferred_element_type=jnp.float32)
    d_input_part, prenorm_grad = back_one(d_norm_one)
    return (
        d_middle + d_input_part,
        (prenorm_grad, heads_grad, mixer_grad, midnorm_grad, expand_grad, reduce_grad),
    )


def local(
    byte_ids,
    seg_ids,
    embed_table,
    slot_project,
    patch_prenorm,
    patch_heads,
    patch_mixer,
    patch_midnorm,
    patch_expand,
    patch_reduce,
    byte_prenorm,
    byte_heads,
    byte_mixer,
    byte_midnorm,
    byte_expand,
    byte_reduce,
    d_output,
):
    slot_count = lax.axis_size("slot")
    slot_index = lax.axis_index("slot")
    group_rows = byte_ids.shape[0]
    own_rows = group_rows // slot_count
    patch_len = byte_ids.shape[1]
    slot_share = patch_len // slot_count
    gathered = (
        lax.all_gather(embed_table, "dp", axis=0, tiled=True),
        lax.all_gather(slot_project, "dp", axis=1, tiled=True),
        lax.all_gather(patch_prenorm, "dp", axis=0, tiled=True),
        lax.all_gather(patch_heads, "dp", axis=0, tiled=True),
        lax.all_gather(patch_mixer, "dp", axis=0, tiled=True),
        lax.all_gather(patch_midnorm, "dp", axis=0, tiled=True),
        lax.all_gather(patch_expand, "dp", axis=0, tiled=True),
        lax.all_gather(patch_reduce, "dp", axis=0, tiled=True),
        lax.all_gather(byte_prenorm, "dp", axis=0, tiled=True),
        lax.all_gather(byte_heads, "dp", axis=0, tiled=True),
        lax.all_gather(byte_mixer, "dp", axis=0, tiled=True),
        lax.all_gather(byte_midnorm, "dp", axis=0, tiled=True),
        lax.all_gather(byte_expand, "dp", axis=0, tiled=True),
        lax.all_gather(byte_reduce, "dp", axis=0, tiled=True),
    )
    lookup = gathered[0]
    project = gathered[1]
    patch_weights = gathered[2:8]
    byte_weights = gathered[8:14]
    vocab_size = lookup.shape[0]
    width = lookup.shape[1]
    head_count = width // HEAD_DIM
    vocab_iota = jnp.arange(vocab_size, dtype=jnp.int32)
    slot_bytes = lax.dynamic_slice_in_dim(byte_ids, slot_index * slot_share, slot_share, 1)
    slot_onehot = (slot_bytes[:, :, None] == vocab_iota).astype(jnp.bfloat16)
    slot_embed = jnp.einsum(
        "gpv,vd->gpd", slot_onehot, lookup, preferred_element_type=jnp.float32
    ).astype(jnp.bfloat16)
    rows_embed = slot_embed
    patch_start = lax.psum_scatter(
        jnp.einsum("cpd,pde->ce", rows_embed, project, preferred_element_type=jnp.float32).astype(
            jnp.bfloat16
        ),
        "slot",
        scatter_dimension=0,
        tiled=True,
    ).astype(jnp.float32)
    segments = seg_ids[0]
    first_row = slot_index * own_rows
    query_pos = first_row + jnp.arange(own_rows, dtype=jnp.int32)
    key_pos = jnp.arange(group_rows, dtype=jnp.int32)
    query_seg = lax.dynamic_slice_in_dim(segments, first_row, own_rows, 0)
    allowed_patch = (
        (query_pos[:, None] >= key_pos[None, :]) & (query_seg[:, None] == segments[None, :])
    )[None]

    def attend_patch(queries, keyset, valueset):
        all_keys, all_values = (
            lax.all_gather(keyset.reshape(own_rows, width), "slot", axis=0, tiled=True),
            lax.all_gather(valueset.reshape(own_rows, width), "slot", axis=0, tiled=True),
        )
        all_keys = all_keys.reshape(1, group_rows, head_count, HEAD_DIM)
        all_values = all_values.reshape(1, group_rows, head_count, HEAD_DIM)
        mixture, logsum = attention(queries, all_keys, all_values, allowed_patch)
        return (mixture, (all_keys, all_values, logsum))

    def attend_patch_back(queries, keyset, valueset, kept, d_mixture):
        all_keys, all_values, logsum = kept
        d_queries, d_keys, d_values = attention_back(
            queries, all_keys, all_values, allowed_patch, logsum, d_mixture
        )
        own_keys, own_values = (
            lax.psum_scatter(
                d_keys.reshape(group_rows, width).astype(jnp.bfloat16),
                "slot",
                scatter_dimension=0,
                tiled=True,
            ).astype(jnp.float32),
            lax.psum_scatter(
                d_values.reshape(group_rows, width).astype(jnp.bfloat16),
                "slot",
                scatter_dimension=0,
                tiled=True,
            ).astype(jnp.float32),
        )
        return (d_queries, own_keys.reshape(keyset.shape), own_values.reshape(valueset.shape))

    patch_out, patch_saved = block_forward(patch_start[None], patch_weights, attend_patch)
    local_bytes = lax.dynamic_slice_in_dim(byte_ids, first_row, own_rows, 0)
    local_onehot = (local_bytes[:, :, None] == vocab_iota).astype(jnp.bfloat16)
    local_embed = jnp.einsum(
        "rpv,vd->rpd", local_onehot, lookup, preferred_element_type=jnp.float32
    )
    fine_input = local_embed + patch_out[0][:, None, :]
    tile_len = math.gcd(own_rows * patch_len, 128)
    tile_count = own_rows * patch_len // tile_len
    fine_input = fine_input.reshape(tile_count, tile_len, width)
    positions = jnp.arange(tile_len, dtype=jnp.int32)
    allowed_byte = (
        (positions[:, None] >= positions[None, :])
        & (positions[:, None] // patch_len == positions[None, :] // patch_len)
    )[None]

    def attend_byte(queries, keyset, valueset):
        return attention(queries, keyset, valueset, allowed_byte)

    def attend_byte_back(queries, keyset, valueset, kept, d_mixture):
        return attention_back(queries, keyset, valueset, allowed_byte, kept, d_mixture)

    byte_out, byte_saved = block_forward(fine_input, byte_weights, attend_byte)
    out_bytes = byte_out.reshape(own_rows, patch_len, width).astype(jnp.bfloat16)
    d_fine, byte_grads = block_backward(
        d_output.astype(jnp.float32).reshape(tile_count, tile_len, width),
        byte_weights,
        byte_saved,
        attend_byte_back,
    )
    d_fine = d_fine.reshape(own_rows, patch_len, width)
    d_patch = jnp.sum(d_fine, axis=1)[None]
    d_start, patch_grads = block_backward(d_patch, patch_weights, patch_saved, attend_patch_back)
    embed_local = jnp.einsum(
        "rpv,rpd->vd", local_onehot.astype(jnp.float32), d_fine, precision=lax.Precision.HIGHEST
    )
    portion = lax.all_gather(d_start[0].astype(jnp.bfloat16), "slot", axis=0, tiled=True)
    rows_embed = slot_embed
    rows_hot = slot_onehot.astype(jnp.float32)
    proj_sum = jnp.einsum("cpd,ce->pde", rows_embed, portion, preferred_element_type=jnp.float32)
    d_rows = jnp.einsum("ce,pde->cpd", portion, project, preferred_element_type=jnp.float32)
    table_sum = jnp.einsum("cpv,cpd->vd", rows_hot, d_rows, precision=lax.Precision.HIGHEST)
    table_grad = embed_local + table_sum
    patch_pre, patch_qkv_grad, patch_mix, patch_mid, patch_exp, patch_red = patch_grads
    byte_pre, byte_qkv_grad, byte_mix, byte_mid, byte_exp, byte_red = byte_grads
    reduced = (
        lax.psum_scatter(table_grad, "dp", scatter_dimension=0, tiled=True),
        lax.psum_scatter(patch_pre, "dp", scatter_dimension=0, tiled=True),
        lax.psum_scatter(patch_qkv_grad, "dp", scatter_dimension=0, tiled=True),
        lax.psum_scatter(patch_mix, "dp", scatter_dimension=0, tiled=True),
        lax.psum_scatter(patch_mid, "dp", scatter_dimension=0, tiled=True),
        lax.psum_scatter(patch_exp, "dp", scatter_dimension=0, tiled=True),
        lax.psum_scatter(patch_red, "dp", scatter_dimension=0, tiled=True),
        lax.psum_scatter(byte_pre, "dp", scatter_dimension=0, tiled=True),
        lax.psum_scatter(byte_qkv_grad, "dp", scatter_dimension=0, tiled=True),
        lax.psum_scatter(byte_mix, "dp", scatter_dimension=0, tiled=True),
        lax.psum_scatter(byte_mid, "dp", scatter_dimension=0, tiled=True),
        lax.psum_scatter(byte_exp, "dp", scatter_dimension=0, tiled=True),
        lax.psum_scatter(byte_red, "dp", scatter_dimension=0, tiled=True),
        lax.psum_scatter(proj_sum, "dp", scatter_dimension=1, tiled=True),
    )
    shares = (
        lax.psum_scatter(
            reduced[0].astype(jnp.bfloat16), "slot", scatter_dimension=0, tiled=True
        ).astype(jnp.float32),
        lax.psum_scatter(
            reduced[1].astype(jnp.bfloat16), "slot", scatter_dimension=0, tiled=True
        ).astype(jnp.float32),
        lax.psum_scatter(
            reduced[2].astype(jnp.bfloat16), "slot", scatter_dimension=0, tiled=True
        ).astype(jnp.float32),
        lax.psum_scatter(
            reduced[3].astype(jnp.bfloat16), "slot", scatter_dimension=0, tiled=True
        ).astype(jnp.float32),
        lax.psum_scatter(
            reduced[4].astype(jnp.bfloat16), "slot", scatter_dimension=0, tiled=True
        ).astype(jnp.float32),
        lax.psum_scatter(
            reduced[5].astype(jnp.bfloat16), "slot", scatter_dimension=0, tiled=True
        ).astype(jnp.float32),
        lax.psum_scatter(
            reduced[6].astype(jnp.bfloat16), "slot", scatter_dimension=0, tiled=True
        ).astype(jnp.float32),
        lax.psum_scatter(
            reduced[7].astype(jnp.bfloat16), "slot", scatter_dimension=0, tiled=True
        ).astype(jnp.float32),
        lax.psum_scatter(
            reduced[8].astype(jnp.bfloat16), "slot", scatter_dimension=0, tiled=True
        ).astype(jnp.float32),
        lax.psum_scatter(
            reduced[9].astype(jnp.bfloat16), "slot", scatter_dimension=0, tiled=True
        ).astype(jnp.float32),
        lax.psum_scatter(
            reduced[10].astype(jnp.bfloat16), "slot", scatter_dimension=0, tiled=True
        ).astype(jnp.float32),
        lax.psum_scatter(
            reduced[11].astype(jnp.bfloat16), "slot", scatter_dimension=0, tiled=True
        ).astype(jnp.float32),
        lax.psum_scatter(
            reduced[12].astype(jnp.bfloat16), "slot", scatter_dimension=0, tiled=True
        ).astype(jnp.float32),
    )
    summed = (
        lax.all_gather(shares[0].astype(jnp.bfloat16), "slot", axis=0, tiled=True).astype(
            jnp.float32
        ),
        lax.all_gather(shares[1].astype(jnp.bfloat16), "slot", axis=0, tiled=True).astype(
            jnp.float32
        ),
        lax.all_gather(shares[2].astype(jnp.bfloat16), "slot", axis=0, tiled=True).astype(
            jnp.float32
        ),
        lax.all_gather(shares[3].astype(jnp.bfloat16), "slot", axis=0, tiled=True).astype(
            jnp.float32
        ),
        lax.all_gather(shares[4].astype(jnp.bfloat16), "slot", axis=0, tiled=True).astype(
            jnp.float32
        ),
        lax.all_gather(shares[5].astype(jnp.bfloat16), "slot", axis=0, tiled=True).astype(
            jnp.float32
        ),
        lax.all_gather(shares[6].astype(jnp.bfloat16), "slot", axis=0, tiled=True).astype(
            jnp.float32
        ),
        lax.all_gather(shares[7].astype(jnp.bfloat16), "slot", axis=0, tiled=True).astype(
            jnp.float32
        ),
        lax.all_gather(shares[8].astype(jnp.bfloat16), "slot", axis=0, tiled=True).astype(
            jnp.float32
        ),
        lax.all_gather(shares[9].astype(jnp.bfloat16), "slot", axis=0, tiled=True).astype(
            jnp.float32
        ),
        lax.all_gather(shares[10].astype(jnp.bfloat16), "slot", axis=0, tiled=True).astype(
            jnp.float32
        ),
        lax.all_gather(shares[11].astype(jnp.bfloat16), "slot", axis=0, tiled=True).astype(
            jnp.float32
        ),
        lax.all_gather(shares[12].astype(jnp.bfloat16), "slot", axis=0, tiled=True).astype(
            jnp.float32
        ),
    )
    proj_final = reduced[13]
    return (
        out_bytes,
        summed[0],
        proj_final,
        summed[1],
        summed[2],
        summed[3],
        summed[4],
        summed[5],
        summed[6],
        summed[7],
        summed[8],
        summed[9],
        summed[10],
        summed[11],
        summed[12],
    )


def solution(mesh):
    placed = (
        P("dp", None),
        P("dp", None),
        P("dp", None),
        P("slot", "dp", None),
        P("dp"),
        P("dp", None),
        P("dp", None),
        P("dp"),
        P("dp", None),
        P("dp", None),
        P("dp"),
        P("dp", None),
        P("dp", None),
        P("dp"),
        P("dp", None),
        P("dp", None),
        P(("dp", "slot"), None, None),
    )
    return jax.shard_map(
        local,
        mesh=mesh,
        in_specs=placed,
        out_specs=(
            P(("dp", "slot"), None, None),
            P("dp", None),
            P("slot", "dp", None),
            P("dp"),
            P("dp", None),
            P("dp", None),
            P("dp"),
            P("dp", None),
            P("dp", None),
            P("dp"),
            P("dp", None),
            P("dp", None),
            P("dp"),
            P("dp", None),
            P("dp", None),
        ),
        check_vma=False,
    )
```

profile of v0, /device:TPU:5, one launch (start us, length us, event | category | flops | bytes accessed | tf_op | source)
XLA Modules:
  0.0 2177.4 jit_solution(748440649385782808)
XLA Ops:
  8.0 26.3 %all_gather.90 = bf16[256,768]{1,0:T(8,128)(2,1)S(1)} all-gather(bf16[32,768]{1,0:T(8,128)(2,1)} %param.19), channel_id=1, replica_groups=mesh['dp'=8,'slot'=4] {'dp'}, dimensions={0}, use_global_device_ids=true | all-gather | bytes 442368 | tf_op jit(solution)/shard_map/all_gather | solution.py:159
  34.8 28.8 %all-gather.10.cloned.1.call-done = bf16[2,768,768]{2,1,0:T(8,128)(2,1)} async-done(((bf16[2,96,768]{2,1,0:T(8,128)(2,1)}), bf16[2,768,768]{2,1,0:T(8,128)(2,1)}) %all-gather.10.cloned.1.call-update) | async-done | bytes 2359312 | tf_op jit(solution)/shard_map/all_gather | solution.py:160
  74.1 16.5 all-reduce.17
  94.1 58.4 %all-gather.12.cloned.1.call-done = bf16[768,2304]{1,0:T(8,128)(2,1)} async-done(((bf16[96,2304]{1,0:T(8,128)(2,1)}), bf16[768,2304]{1,0:T(8,128)(2,1)}) %all-gather.12.cloned.1.call-update) | async-done | bytes 3538960 | tf_op jit(solution)/shard_map/all_gather | solution.py:162
  155.8 7.1 all_gather.94
  163.2 5.6 all_gather.95
  170.0 23.9 %all-gather.14.cloned.1.call-done = bf16[768,768]{1,0:T(8,128)(2,1)} async-done(((bf16[96,768]{1,0:T(8,128)(2,1)}), bf16[768,768]{1,0:T(8,128)(2,1)}) %all-gather.14.cloned.1.call-update) | async-done | bytes 1179664 | tf_op jit(solution)/shard_map/all_gather | solution.py:163
  196.5 78.4 %all-gather.16.cloned.1.call-done = bf16[768,3072]{1,0:T(8,128)(2,1)} async-done(((bf16[96,3072]{1,0:T(8,128)(2,1)}), bf16[768,3072]{1,0:T(8,128)(2,1)}) %all-gather.16.cloned.1.call-update) | async-done | bytes 4718608 | tf_op jit(solution)/shard_map/all_gather | solution.py:165
  278.2 76.8 %all-gather.18.cloned.1.call-done = bf16[3072,768]{1,0:T(8,128)(2,1)} async-done(((bf16[384,768]{1,0:T(8,128)(2,1)}), bf16[3072,768]{1,0:T(8,128)(2,1)}) %all-gather.18.cloned.1.call-update) | async-done | bytes 4718608 | tf_op jit(solution)/shard_map/all_gather | solution.py:166
  360.4 60.1 %all-gather.20.cloned.1.call-done = bf16[768,2304]{1,0:T(8,128)(2,1)} async-done(((bf16[96,2304]{1,0:T(8,128)(2,1)}), bf16[768,2304]{1,0:T(8,128)(2,1)}) %all-gather.20.cloned.1.call-update) | async-done | bytes 3538960 | tf_op jit(solution)/shard_map/all_gather | solution.py:168
  429.4 32.6 %all-gather.22.cloned.1.call-done = bf16[768,768]{1,0:T(8,128)(2,1)} async-done(((bf16[96,768]{1,0:T(8,128)(2,1)}), bf16[768,768]{1,0:T(8,128)(2,1)}) %all-gather.22.cloned.1.call-update) | async-done | bytes 1179664 | tf_op jit(solution)/shard_map/all_gather | solution.py:169
  466.6 76.6 %all-gather.24.cloned.1.call-done = bf16[768,3072]{1,0:T(8,128)(2,1)} async-done(((bf16[96,3072]{1,0:T(8,128)(2,1)}), bf16[768,3072]{1,0:T(8,128)(2,1)}) %all-gather.24.cloned.1.call-update) | async-done | bytes 4718608 | tf_op jit(solution)/shard_map/all_gather | solution.py:171
  543.1 5.5 fusion.6
  548.6 74.6 %all-gather.26.cloned.1.call-done = bf16[3072,768]{1,0:T(8,128)(2,1)} async-done(((bf16[384,768]{1,0:T(8,128)(2,1)}), bf16[3072,768]{1,0:T(8,128)(2,1)}) %all-gather.26.cloned.1.call-update) | async-done | bytes 4718608 | tf_op jit(solution)/shard_map/all_gather | solution.py:172
  623.2 6.8 fusion.15
  668.2 13.8 reduce-scatter.27.cloned.1.call-done
  683.0 21.6 reduce-scatter.25.cloned.1.call-done
  710.4 6.1 all_gather.106
  753.9 7.8 convolution_bitcast_fusion
  761.8 19.6 reduce-scatter.29.cloned.1.call-done
  783.0 70.9 %reduce-scatter.39.cloned.1.call-done = f32[96,768]{1,0:T(8,128)} async-done(((f32[768,768]{1,0:T(8,128)}), f32[96,768]{1,0:T(8,128)}) %reduce-scatter.39.cloned.1.call-update) | async-done | bytes 294928 | tf_op jit(solution)/shard_map/reduce_scatter | solution.py:285
  855.5 70.1 %reduce-scatter.55.cloned.1.call-done = f32[96,768]{1,0:T(8,128)} async-done(((f32[768,768]{1,0:T(8,128)}), f32[96,768]{1,0:T(8,128)}) %reduce-scatter.55.cloned.1.call-update) | async-done | bytes 294928 | tf_op jit(solution)/shard_map/reduce_scatter | solution.py:291
  927.3 130.5 %reduce-scatter.51.cloned.1.call-done = f32[96,2304]{1,0:T(8,128)} async-done(((f32[768,2304]{1,0:T(8,128)}), f32[96,2304]{1,0:T(8,128)}) %reduce-scatter.51.cloned.1.call-update) | async-done | bytes 884752 | tf_op jit(solution)/shard_map/reduce_scatter | solution.py:290
  1059.8 129.6 %reduce-scatter.35.cloned.1.call-done = f32[96,2304]{1,0:T(8,128)} async-done(((f32[768,2304]{1,0:T(8,128)}), f32[96,2304]{1,0:T(8,128)}) %reduce-scatter.35.cloned.1.call-update) | async-done | bytes 884752 | tf_op jit(solution)/shard_map/reduce_scatter | solution.py:284
  1191.5 165.3 %reduce-scatter.43.cloned.1.call-done = f32[96,3072]{1,0:T(8,128)} async-done(((f32[768,3072]{1,0:T(8,128)}), f32[96,3072]{1,0:T(8,128)}) %reduce-scatter.43.cloned.1.call-update) | async-done | bytes 1179664 | tf_op jit(solution)/shard_map/reduce_scatter | solution.py:287
  1359.0 164.4 %reduce-scatter.47.cloned.1.call-done = f32[384,768]{1,0:T(8,128)} async-done(((f32[3072,768]{1,0:T(8,128)}), f32[384,768]{1,0:T(8,128)}) %reduce-scatter.47.cloned.1.call-update) | async-done | bytes 1179664 | tf_op jit(solution)/shard_map/reduce_scatter | solution.py:288
  1525.6 164.3 %reduce-scatter.59.cloned.1.call-done = f32[96,3072]{1,0:T(8,128)} async-done(((f32[768,3072]{1,0:T(8,128)}), f32[96,3072]{1,0:T(8,128)}) %reduce-scatter.59.cloned.1.call-update) | async-done | bytes 1179664 | tf_op jit(solution)/shard_map/reduce_scatter | solution.py:293
  1692.1 164.4 %reduce-scatter.63.cloned.1.call-done = f32[384,768]{1,0:T(8,128)} async-done(((f32[3072,768]{1,0:T(8,128)}), f32[384,768]{1,0:T(8,128)}) %reduce-scatter.63.cloned.1.call-update) | async-done | bytes 1179664 | tf_op jit(solution)/shard_map/reduce_scatter | solution.py:294
  1863.7 6.0 fusion.28
  1869.8 28.1 %all-reduce.16 = (bf16[768]{0:T(1024)(128)(2,1)S(1)}, bf16[768]{0:T(1024)(128)(2,1)S(1)}, bf16[768]{0:T(1024)(128)(2,1)S(1)}, bf16[768]{0:T(1024)(128)(2,1)S(1)}) all-reduce(f32[768]{0:T(1024)S(1)} %copy-done.64, f32[768]{0:T(1024)S(1)} %copy-done.65, f32[768]{0:T(1024)S(1)} %copy-done.60, ...), channel_id=8, replica_groups=mesh['dp'=8,'slot'=4] {'dp'}, use_global_device_ids=true, to_apply=%region_30.31.clone | all-reduce | flops 3072 | bytes 18432
  1898.2 12.7 all-reduce.19
  1912.0 5.9 all-reduce.18
  1919.9 6.0 all_gather.107
  1926.6 5.9 all_gather.110
  1933.2 5.7 all_gather.116
  1939.6 7.0 reduce-scatter.53.cloned.1.call-done
  1946.6 7.5 all_gather.115
  1955.1 15.6 reduce-scatter.37.cloned.1.call-done
  1970.7 7.5 all_gather.109
  1979.2 16.5 reduce-scatter.45.cloned.1.call-done
  1995.7 8.3 all_gather.112
  2005.1 15.7 reduce-scatter.49.cloned.1.call-done
  2020.9 8.4 all_gather.113
  2030.4 15.1 reduce-scatter.61.cloned.1.call-done
  2045.5 8.3 all_gather.118
  2054.9 15.0 reduce-scatter.65.cloned.1.call-done
  2069.9 8.3 all_gather.119
  2079.3 91.1 %reduce-scatter.33.cloned.1.call-done = f32[2,96,768]{2,1,0:T(8,128)} async-done(((f32[2,768,768]{2,1,0:T(8,128)}), f32[2,96,768]{2,1,0:T(8,128)}) %reduce-scatter.33.cloned.1.call-update) | async-done | bytes 589840 | tf_op jit(solution)/shard_map/reduce_scatter | solution.py:295
  (418 shorter events, 157.8 us)
Async XLA Ops:
  7.2 56.4 %all-gather.10.cloned.1.call-start = ((), (), s32[]{:S(2)}) async-start(), calls=%async_computation.22 | async-start | bytes 2654208 | tf_op jit(solution)/shard_map/all_gather | solution.py:160
  7.9 83.8 %reduce-scatter.23.cloned.1.call-start = ((), (), s32[]{:S(2)}) async-start(), calls=%async_computation.23 | async-start | bytes 245760 | tf_op jit(solution)/shard_map/reduce_scatter | solution.py:188
  8.0 61.6 %copy-start.78 = (s32[128,2]{0,1:T(2,128)}, s32[128,2]{0,1:T(2,128)S(1)}, u32[]{:S(2)}) copy-start(s32[128,2]{0,1:T(2,128)S(1)} %constant_dynamic-slice_fusion.1) | copy-start | bytes 3076
  34.8 56.0 %copy-start.89 = (s32[1,128]{1,0:T(1,128)S(1)}, s32[1,128]{1,0:T(1,128)}, u32[]{:S(2)}) copy-start(s32[1,128]{1,0:T(1,128)} %param.18) | copy-start | bytes 1540
  66.4 86.1 %all-gather.12.cloned.1.call-start = ((), (), s32[]{:S(2)}) async-start(), calls=%async_computation.24 | async-start | bytes 3981312 | tf_op jit(solution)/shard_map/all_gather | solution.py:162
  67.2 126.7 %all-gather.14.cloned.1.call-start = ((), (), s32[]{:S(2)}) async-start(), calls=%async_computation.25 | async-start | bytes 1327104 | tf_op jit(solution)/shard_map/all_gather | solution.py:163
  67.7 207.1 %all-gather.16.cloned.1.call-start = ((), (), s32[]{:S(2)}) async-start(), calls=%async_computation.26 | async-start | bytes 5308416 | tf_op jit(solution)/shard_map/all_gather | solution.py:165
  68.3 286.6 %all-gather.18.cloned.1.call-start = ((), (), s32[]{:S(2)}) async-start(), calls=%async_computation.27 | async-start | bytes 5308416 | tf_op jit(solution)/shard_map/all_gather | solution.py:166
  68.9 351.6 %all-gather.20.cloned.1.call-start = ((), (), s32[]{:S(2)}) async-start(), calls=%async_computation.28 | async-start | bytes 3981312 | tf_op jit(solution)/shard_map/all_gather | solution.py:168
  69.7 392.3 %all-gather.22.cloned.1.call-start = ((), (), s32[]{:S(2)}) async-start(), calls=%async_computation.29 | async-start | bytes 1327104 | tf_op jit(solution)/shard_map/all_gather | solution.py:169
  70.4 472.7 %all-gather.24.cloned.1.call-start = ((), (), s32[]{:S(2)}) async-start(), calls=%async_computation.30 | async-start | bytes 5308416 | tf_op jit(solution)/shard_map/all_gather | solution.py:171
  71.1 552.1 %all-gather.26.cloned.1.call-start = ((), (), s32[]{:S(2)}) async-start(), calls=%async_computation.31 | async-start | bytes 5308416 | tf_op jit(solution)/shard_map/all_gather | solution.py:172
  71.7 610.2 %reduce-scatter.27.cloned.1.call-start = ((), (), s32[]{:S(2)}) async-start(), calls=%async_computation.33 | async-start | bytes 245760 | tf_op jit(solution)/shard_map/reduce_scatter | solution.py:227
  92.7 62.7 %copy-start.54 = (f32[32]{0:T(128)}, f32[32]{0:T(128)S(1)}, u32[]{:S(2)}) copy-start(f32[32]{0:T(128)S(1)} %broadcast_multiply_fusion.3) | copy-start | bytes 388
  94.1 74.7 %copy-start.68 = (f32[32]{0:T(128)}, f32[32]{0:T(128)S(1)}, u32[]{:S(2)}) copy-start(f32[32]{0:T(128)S(1)} %fusion.95) | copy-start | bytes 388
  155.7 122.5 %copy-start.35 = (bf16[1,32,1,12,64]{4,3,2,1,0:T(8,128)(2,1)}, bf16[1,32,1,12,64]{4,3,2,1,0:T(8,128)(2,1)S(1)}, u32[]{:S(2)}) copy-start(bf16[1,32,1,12,64]{4,3,2,1,0:T(8,128)(2,1)S(1)} %get-tuple-element.43) | copy-start | bytes 147460
  163.1 115.1 %copy-start.36 = (bf16[128,768]{0,1:T(8,128)(2,1)}, bf16[128,768]{0,1:T(8,128)(2,1)S(1)}, u32[]{:S(2)}) copy-start(bf16[128,768]{0,1:T(8,128)(2,1)S(1)} %copy.87) | copy-start | bytes 589828
  169.0 109.2 %copy-start.24 = (bf16[128,768]{0,1:T(8,128)(2,1)}, bf16[128,768]{0,1:T(8,128)(2,1)S(1)}, u32[]{:S(2)}) copy-start(bf16[128,768]{0,1:T(8,128)(2,1)S(1)} %copy.89) | copy-start | bytes 589828
  170.0 108.2 %copy-start.37 = (bf16[32,768]{1,0:T(8,128)(2,1)}, bf16[32,768]{1,0:T(8,128)(2,1)S(1)}, u32[]{:S(2)}) copy-start(bf16[32,768]{1,0:T(8,128)(2,1)S(1)} %reshape.673) | copy-start | bytes 147460
  195.6 162.6 %copy-start.5 = (f32[32,768]{1,0:T(8,128)}, f32[32,768]{1,0:T(8,128)S(1)}, u32[]{:S(2)}) copy-start(f32[32,768]{1,0:T(8,128)S(1)} %get-tuple-element.55) | copy-start | bytes 294916
  195.6 159.3 %copy-start.57 = (f32[32]{0:T(128)}, f32[32]{0:T(128)S(1)}, u32[]{:S(2)}) copy-start(f32[32]{0:T(128)S(1)} %broadcast_multiply_fusion.2) | copy-start | bytes 388
  195.8 159.2 %copy-start.87 = (f32[32]{0:T(128)}, f32[32]{0:T(128)S(1)}, u32[]{:S(2)}) copy-start(f32[32]{0:T(128)S(1)} %multiply_reduce_fusion.10) | copy-start | bytes 388
  195.8 159.1 %copy-start.71 = (f32[32]{0:T(128)}, f32[32]{0:T(128)S(1)}, u32[]{:S(2)}) copy-start(f32[32]{0:T(128)S(1)} %fusion.96) | copy-start | bytes 388
  358.6 65.0 %copy-start.40 = (f32[32,8]{1,0:T(8,128)}, f32[32,8]{1,0:T(8,128)S(1)}, u32[]{:S(2)}) copy-start(f32[32,8]{1,0:T(8,128)S(1)} %broadcast_multiply_fusion) | copy-start | bytes 3076
  358.7 65.0 %copy-start.52 = (f32[2,128]{1,0:T(2,128)}, f32[2,128]{1,0:T(2,128)S(1)}, u32[]{:S(2)}) copy-start(f32[2,128]{1,0:T(2,128)S(1)} %div.112) | copy-start | bytes 3076
  360.4 64.9 %copy-start.63 = (pred[128,128]{0,1:T(8,128)(4,1)S(1)}, pred[128,128]{0,1:T(8,128)(4,1)}, u32[]{:S(2)}) copy-start(pred[128,128]{0,1:T(8,128)(4,1)} %fusion.82) | copy-start | bytes 49156
  664.1 40.5 %reduce-scatter.25.cloned.1.call-start = ((), (), s32[]{:S(2)}) async-start(), calls=%async_computation.32 | async-start | bytes 245760 | tf_op jit(solution)/shard_map/reduce_scatter | solution.py:221
  667.0 114.4 %reduce-scatter.29.cloned.1.call-start = ((), (), s32[]{:S(2)}) async-start(), calls=%async_computation.34 | async-start | bytes 884736 | tf_op jit(solution)/shard_map/reduce_scatter | solution.py:282
  719.8 134.0 %reduce-scatter.39.cloned.1.call-start = ((), (), s32[]{:S(2)}) async-start(), calls=%async_computation.39 | async-start | bytes 2654208 | tf_op jit(solution)/shard_map/reduce_scatter | solution.py:285
  721.9 203.7 %reduce-scatter.55.cloned.1.call-start = ((), (), s32[]{:S(2)}) async-start(), calls=%async_computation.47 | async-start | bytes 2654208 | tf_op jit(solution)/shard_map/reduce_scatter | solution.py:291
  725.0 332.8 %reduce-scatter.51.cloned.1.call-start = ((), (), s32[]{:S(2)}) async-start(), calls=%async_computation.45 | async-start | bytes 7962624 | tf_op jit(solution)/shard_map/reduce_scatter | solution.py:290
  729.3 460.1 %reduce-scatter.35.cloned.1.call-start = ((), (), s32[]{:S(2)}) async-start(), calls=%async_computation.37 | async-start | bytes 7962624 | tf_op jit(solution)/shard_map/reduce_scatter | solution.py:284
  734.3 622.5 %reduce-scatter.43.cloned.1.call-start = ((), (), s32[]{:S(2)}) async-start(), calls=%async_computation.41 | async-start | bytes 10616832 | tf_op jit(solution)/shard_map/reduce_scatter | solution.py:287
  740.3 783.1 %reduce-scatter.47.cloned.1.call-start = ((), (), s32[]{:S(2)}) async-start(), calls=%async_computation.43 | async-start | bytes 10616832 | tf_op jit(solution)/shard_map/reduce_scatter | solution.py:288
  746.3 943.6 %reduce-scatter.59.cloned.1.call-start = ((), (), s32[]{:S(2)}) async-start(), calls=%async_computation.49 | async-start | bytes 10616832 | tf_op jit(solution)/shard_map/reduce_scatter | solution.py:293
  753.0 1103.6 %reduce-scatter.63.cloned.1.call-start = ((), (), s32[]{:S(2)}) async-start(), calls=%async_computation.51 | async-start | bytes 10616832 | tf_op jit(solution)/shard_map/reduce_scatter | solution.py:294
  761.7 1158.2 %reduce-scatter.31.cloned.1.call-start = ((), (), s32[]{:S(2)}) async-start(), calls=%async_computation.35 | async-start | bytes 61440 | tf_op jit(solution)/shard_map/reduce_scatter | solution.py:298
  782.9 1143.6 %reduce-scatter.41.cloned.1.call-start = ((), (), s32[]{:S(2)}) async-start(), calls=%async_computation.40 | async-start | bytes 184320 | tf_op jit(solution)/shard_map/reduce_scatter | solution.py:307
  855.5 1077.7 %reduce-scatter.57.cloned.1.call-start = ((), (), s32[]{:S(2)}) async-start(), calls=%async_computation.48 | async-start | bytes 184320 | tf_op jit(solution)/shard_map/reduce_scatter | solution.py:325
  927.3 1019.3 %reduce-scatter.53.cloned.1.call-start = ((), (), s32[]{:S(2)}) async-start(), calls=%async_computation.46 | async-start | bytes 552960 | tf_op jit(solution)/shard_map/reduce_scatter | solution.py:322
  1059.8 910.9 %reduce-scatter.37.cloned.1.call-start = ((), (), s32[]{:S(2)}) async-start(), calls=%async_computation.38 | async-start | bytes 552960 | tf_op jit(solution)/shard_map/reduce_scatter | solution.py:304
  1191.4 804.3 %reduce-scatter.45.cloned.1.call-start = ((), (), s32[]{:S(2)}) async-start(), calls=%async_computation.42 | async-start | bytes 737280 | tf_op jit(solution)/shard_map/reduce_scatter | solution.py:313
  1359.0 499.8 %copy-start.22 = (bf16[128,2,768]{2,0,1:T(8,128)(2,1)S(1)}, bf16[128,2,768]{2,0,1:T(8,128)(2,1)}, u32[]{:S(2)}) copy-start(bf16[128,2,768]{2,0,1:T(8,128)(2,1)} %copy-done.21) | copy-start | bytes 1179652
  1359.0 661.9 %reduce-scatter.49.cloned.1.call-start = ((), (), s32[]{:S(2)}) async-start(), calls=%async_computation.44 | async-start | bytes 737280 | tf_op jit(solution)/shard_map/reduce_scatter | solution.py:316
  1525.6 519.9 %reduce-scatter.61.cloned.1.call-start = ((), (), s32[]{:S(2)}) async-start(), calls=%async_computation.50 | async-start | bytes 737280 | tf_op jit(solution)/shard_map/reduce_scatter | solution.py:331
  1692.1 377.8 %reduce-scatter.65.cloned.1.call-start = ((), (), s32[]{:S(2)}) async-start(), calls=%async_computation.52 | async-start | bytes 737280 | tf_op jit(solution)/shard_map/reduce_scatter | solution.py:334
  1858.7 311.7 %reduce-scatter.33.cloned.1.call-start = ((), (), s32[]{:S(2)}) async-start(), calls=%async_computation.36 | async-start | bytes 5308416 | tf_op jit(solution)/shard_map/reduce_scatter | solution.py:295
  2020.9 149.5 %copy-start.1 = (s32[128,8]{0,1:T(8,128)S(1)}, s32[128,8]{0,1:T(8,128)}, u32[]{:S(2)}) copy-start(s32[128,8]{0,1:T(8,128)} %param.17) | copy-start | bytes 12292
  (78 other events, 682.3 us)
Sparse Core Ops, SparseCore 0:
  10.2 53.3 all-gather.9
  66.6 18.3 reduce-scatter.22
  87.2 65.3 all-gather.11
  154.6 39.2 all-gather.13
  195.9 78.9 all-gather.15
  276.9 78.0 all-gather.17
  357.1 63.3 all-gather.19
  422.7 39.2 all-gather.21
  464.2 78.9 all-gather.23
  545.2 78.0 all-gather.25
  664.2 17.7 reduce-scatter.26
  684.8 19.7 reduce-scatter.24
  719.9 61.3 reduce-scatter.28
  785.1 68.6 reduce-scatter.38
  857.6 67.9 reduce-scatter.54
  929.6 128.1 reduce-scatter.50
  1061.3 128.0 reduce-scatter.34
  1193.3 163.4 reduce-scatter.42
  1360.8 162.5 reduce-scatter.46
  1527.3 162.5 reduce-scatter.58
  1693.9 162.5 reduce-scatter.62
  1859.7 16.8 reduce-scatter.30
  1879.5 19.9 reduce-scatter.40
  1902.4 19.6 reduce-scatter.56
  1925.2 21.4 reduce-scatter.52
  1949.6 21.1 reduce-scatter.36
  1973.6 22.0 reduce-scatter.44
  1998.8 22.0 reduce-scatter.48
  2023.4 22.0 reduce-scatter.60
  2047.8 22.0 reduce-scatter.64
  2074.1 96.2 reduce-scatter.32
where the time goes:
time: 2190 us; the launch traced here: 2180 us
  waiting for transfers between devices  1810 us (83%)
  blocking collectives  174 us (8%)
  matrix products  110 us (5%)
  other arithmetic  42 us (2%)
  local copies, waits for them, and re-layouts  24 us (1%)
    reduce_scatter x1, waiting for transfers between devices, local(): lax.psum_scatter(patch_exp, 'dp', scatter_dimension=0, tiled=True)  165 us
    reduce_scatter x1, waiting for transfers between devices, local(): lax.psum_scatter(byte_red, 'dp', scatter_dimension=0, tiled=True)  164 us
    reduce_scatter x1, waiting for transfers between devices, local(): lax.psum_scatter(patch_red, 'dp', scatter_dimension=0, tiled=True)  164 us
    reduce_scatter x1, waiting for transfers between devices, local(): lax.psum_scatter(byte_exp, 'dp', scatter_dimension=0, tiled=True)  164 us
    reduce_scatter x1, waiting for transfers between devices, local(): lax.psum_scatter(byte_qkv_grad, 'dp', scatter_dimension=0, tiled=True)  130 us
    reduce_scatter x1, waiting for transfers between devices, local(): lax.psum_scatter(patch_qkv_grad, 'dp', scatter_dimension=0, tiled=True)  130 us
    reduce_scatter x1, waiting for transfers between devices, local(): lax.psum_scatter(proj_sum, 'dp', scatter_dimension=1, tiled=True)  91.1 us
    all_gather x1, waiting for transfers between devices, local(): lax.all_gather(patch_expand, 'dp', axis=0, tiled=True)  78.4 us
  transfers between devices with their start and end apart: 31, of which 27 were waited for; matrix products, arithmetic and copies ran while one was open for 5% of the time, Pallas kernels for 0%

commit v1 on v0

v1 whole, which is shorter than its diff:
```python
import functools
import math
from types import SimpleNamespace as NS

import jax
import jax.numpy as jnp
from jax import lax
from jax.experimental import pallas as pl
from jax.experimental.pallas import tpu as pltpu
from jax.sharding import PartitionSpec as P

MESH = pl.DeviceIdType.MESH
BF = jnp.bfloat16
F32 = jnp.float32
DP, SLOT = "dp", "slot"
SHARED, PRIVATE, ZONLY, SINGLE = range(4)

HEAD_DIM = 64


EPSILON = 1e-05
MASKED = -1000000000.0


def norm_rows(values, gain_vec):
    center = jnp.mean(values, axis=-1, keepdims=True)
    shifted = values - center
    spread = jnp.mean(shifted * shifted, axis=-1, keepdims=True)
    return shifted * lax.rsqrt(spread + EPSILON) * gain_vec


def gelu_tanh(values):
    inside = 0.7978845608028654 * (values + 0.044715 * values * values * values)
    return 0.5 * values * (1.0 + jnp.tanh(inside))


def attention(queries, keyset, valueset, allowed):
    scores = jnp.einsum(
        "bnhe,bmhe->bhnm", queries, keyset, preferred_element_type=jnp.float32
    ) * HEAD_DIM ** (-0.5)
    scores = jnp.where(allowed[:, None], scores, MASKED)
    highest = jnp.max(scores, axis=-1, keepdims=True)
    exponents = jnp.exp(scores - highest)
    totals = jnp.sum(exponents, axis=-1, keepdims=True)
    softened = (exponents / totals).astype(jnp.bfloat16)
    mixture = jnp.einsum("bhnm,bmhe->bnhe", softened, valueset, preferred_element_type=jnp.float32)
    return (mixture, highest + jnp.log(totals))


def attention_back(queries, keyset, valueset, allowed, logsum, d_mixture):
    scale_value = HEAD_DIM ** (-0.5)
    scores = (
        jnp.einsum("bnhe,bmhe->bhnm", queries, keyset, preferred_element_type=jnp.float32)
        * scale_value
    )
    scores = jnp.where(allowed[:, None], scores, MASKED)
    softened = jnp.exp(scores - logsum)
    d_soft = jnp.einsum("bnhe,bmhe->bhnm", d_mixture, valueset, preferred_element_type=jnp.float32)
    inside = jnp.sum(d_soft * softened, axis=-1, keepdims=True)
    d_scores = (softened * (d_soft - inside)).astype(jnp.bfloat16)
    d_queries = (
        jnp.einsum("bhnm,bmhe->bnhe", d_scores, keyset, preferred_element_type=jnp.float32)
        * scale_value
    )
    d_keys = (
        jnp.einsum("bhnm,bnhe->bmhe", d_scores, queries, preferred_element_type=jnp.float32)
        * scale_value
    )
    d_values = jnp.einsum(
        "bhnm,bnhe->bmhe",
        softened.astype(jnp.bfloat16),
        d_mixture,
        preferred_element_type=jnp.float32,
    )
    return (d_queries, d_keys, d_values)


def block_forward(values, weights, attend):
    gain_one, w_heads, w_mixer, gain_two, w_expand, w_reduce = weights
    batch, row_count, width = values.shape
    head_count = width // HEAD_DIM
    norm_one, back_one = jax.vjp(norm_rows, values, gain_one.astype(jnp.float32))
    norm_one = norm_one.astype(jnp.bfloat16)
    joined = jnp.einsum(
        "bnd,df->bnf", norm_one, w_heads, preferred_element_type=jnp.float32
    ).astype(jnp.bfloat16)
    joined = joined.reshape(batch, row_count, 3, head_count, HEAD_DIM)
    mixture, kept = attend(joined[:, :, 0], joined[:, :, 1], joined[:, :, 2])
    mixture = mixture.astype(jnp.bfloat16).reshape(batch, row_count, width)
    middle = values + jnp.einsum(
        "bnf,fd->bnd", mixture, w_mixer, preferred_element_type=jnp.float32
    )
    norm_two, back_two = jax.vjp(norm_rows, middle, gain_two.astype(jnp.float32))
    norm_two = norm_two.astype(jnp.bfloat16)
    expanded = jnp.einsum("bnd,df->bnf", norm_two, w_expand, preferred_element_type=jnp.float32)
    hidden, back_gelu = jax.vjp(gelu_tanh, expanded)
    hidden = hidden.astype(jnp.bfloat16)
    result = middle + jnp.einsum(
        "bnf,fd->bnd", hidden, w_reduce, preferred_element_type=jnp.float32
    )
    saved = (back_one, norm_one, joined, kept, mixture, back_two, norm_two, back_gelu, hidden)
    return (result, saved)


def block_backward(grad_out, weights, saved, attend_back):
    gain_one, w_heads, w_mixer, gain_two, w_expand, w_reduce = weights
    back_one, norm_one, joined, kept, mixture, back_two, norm_two, back_gelu, hidden = saved
    batch, row_count, width = grad_out.shape
    grad_low = grad_out.astype(jnp.bfloat16)
    reduce_grad = jnp.einsum("bnf,bnd->fd", hidden, grad_low, preferred_element_type=jnp.float32)
    d_hidden = jnp.einsum("bnd,fd->bnf", grad_low, w_reduce, preferred_element_type=jnp.float32)
    (d_expanded,) = back_gelu(d_hidden)
    d_expanded = d_expanded.astype(jnp.bfloat16)
    expand_grad = jnp.einsum(
        "bnd,bnf->df", norm_two, d_expanded, preferred_element_type=jnp.float32
    )
    d_norm_two = jnp.einsum("bnf,df->bnd", d_expanded, w_expand, preferred_element_type=jnp.float32)
    d_middle_part, midnorm_grad = back_two(d_norm_two)
    d_middle = grad_out + d_middle_part
    middle_low = d_middle.astype(jnp.bfloat16)
    mixer_grad = jnp.einsum("bnf,bnd->fd", mixture, middle_low, preferred_element_type=jnp.float32)
    d_mixture = jnp.einsum(
        "bnd,fd->bnf", middle_low, w_mixer, preferred_element_type=jnp.float32
    ).astype(jnp.bfloat16)
    d_mixture = d_mixture.reshape(batch, row_count, width // HEAD_DIM, HEAD_DIM)
    d_queries, d_keys, d_values = attend_back(
        joined[:, :, 0], joined[:, :, 1], joined[:, :, 2], kept, d_mixture
    )
    d_joined = (
        jnp.stack([d_queries, d_keys, d_values], axis=2)
        .reshape(batch, row_count, 3 * width)
        .astype(jnp.bfloat16)
    )
    heads_grad = jnp.einsum("bnd,bnf->df", norm_one, d_joined, preferred_element_type=jnp.float32)
    d_norm_one = jnp.einsum("bnf,df->bnd", d_joined, w_heads, preferred_element_type=jnp.float32)
    d_input_part, prenorm_grad = back_one(d_norm_one)
    return (
        d_middle + d_input_part,
        (prenorm_grad, heads_grad, mixer_grad, midnorm_grad, expand_grad, reduce_grad),
    )


def generic_local(
    byte_ids,
    seg_ids,
    embed_table,
    slot_project,
    patch_prenorm,
    patch_heads,
    patch_mixer,
    patch_midnorm,
    patch_expand,
    patch_reduce,
    byte_prenorm,
    byte_heads,
    byte_mixer,
    byte_midnorm,
    byte_expand,
    byte_reduce,
    d_output,
):
    slot_count = lax.axis_size(SLOT)
    slot_index = lax.axis_index(SLOT)
    group_rows = byte_ids.shape[0]
    own_rows = group_rows // slot_count
    patch_len = byte_ids.shape[1]
    slot_share = patch_len // slot_count
    gathered = (
        lax.all_gather(embed_table, DP, axis=0, tiled=True),
        lax.all_gather(slot_project, DP, axis=1, tiled=True),
        lax.all_gather(patch_prenorm, DP, axis=0, tiled=True),
        lax.all_gather(patch_heads, DP, axis=0, tiled=True),
        lax.all_gather(patch_mixer, DP, axis=0, tiled=True),
        lax.all_gather(patch_midnorm, DP, axis=0, tiled=True),
        lax.all_gather(patch_expand, DP, axis=0, tiled=True),
        lax.all_gather(patch_reduce, DP, axis=0, tiled=True),
        lax.all_gather(byte_prenorm, DP, axis=0, tiled=True),
        lax.all_gather(byte_heads, DP, axis=0, tiled=True),
        lax.all_gather(byte_mixer, DP, axis=0, tiled=True),
        lax.all_gather(byte_midnorm, DP, axis=0, tiled=True),
        lax.all_gather(byte_expand, DP, axis=0, tiled=True),
        lax.all_gather(byte_reduce, DP, axis=0, tiled=True),
    )
    lookup = gathered[0]
    project = gathered[1]
    patch_weights = gathered[2:8]
    byte_weights = gathered[8:14]
    vocab_size = lookup.shape[0]
    width = lookup.shape[1]
    head_count = width // HEAD_DIM
    vocab_iota = jnp.arange(vocab_size, dtype=jnp.int32)
    slot_bytes = lax.dynamic_slice_in_dim(byte_ids, slot_index * slot_share, slot_share, 1)
    slot_onehot = (slot_bytes[:, :, None] == vocab_iota).astype(jnp.bfloat16)
    slot_embed = jnp.einsum(
        "gpv,vd->gpd", slot_onehot, lookup, preferred_element_type=jnp.float32
    ).astype(jnp.bfloat16)
    rows_embed = slot_embed
    patch_start = lax.psum_scatter(
        jnp.einsum("cpd,pde->ce", rows_embed, project, preferred_element_type=jnp.float32).astype(
            jnp.bfloat16
        ),
        SLOT,
        scatter_dimension=0,
        tiled=True,
    ).astype(jnp.float32)
    segments = seg_ids[0]
    first_row = slot_index * own_rows
    query_pos = first_row + jnp.arange(own_rows, dtype=jnp.int32)
    key_pos = jnp.arange(group_rows, dtype=jnp.int32)
    query_seg = lax.dynamic_slice_in_dim(segments, first_row, own_rows, 0)
    allowed_patch = (
        (query_pos[:, None] >= key_pos[None, :]) & (query_seg[:, None] == segments[None, :])
    )[None]

    def attend_patch(queries, keyset, valueset):
        all_keys, all_values = (
            lax.all_gather(keyset.reshape(own_rows, width), SLOT, axis=0, tiled=True),
            lax.all_gather(valueset.reshape(own_rows, width), SLOT, axis=0, tiled=True),
        )
        all_keys = all_keys.reshape(1, group_rows, head_count, HEAD_DIM)
        all_values = all_values.reshape(1, group_rows, head_count, HEAD_DIM)
        mixture, logsum = attention(queries, all_keys, all_values, allowed_patch)
        return (mixture, (all_keys, all_values, logsum))

    def attend_patch_back(queries, keyset, valueset, kept, d_mixture):
        all_keys, all_values, logsum = kept
        d_queries, d_keys, d_values = attention_back(
            queries, all_keys, all_values, allowed_patch, logsum, d_mixture
        )
        own_keys, own_values = (
            lax.psum_scatter(
                d_keys.reshape(group_rows, width).astype(jnp.bfloat16),
                SLOT,
                scatter_dimension=0,
                tiled=True,
            ).astype(jnp.float32),
            lax.psum_scatter(
                d_values.reshape(group_rows, width).astype(jnp.bfloat16),
                SLOT,
                scatter_dimension=0,
                tiled=True,
            ).astype(jnp.float32),
        )
        return (d_queries, own_keys.reshape(keyset.shape), own_values.reshape(valueset.shape))

    patch_out, patch_saved = block_forward(patch_start[None], patch_weights, attend_patch)
    local_bytes = lax.dynamic_slice_in_dim(byte_ids, first_row, own_rows, 0)
    local_onehot = (local_bytes[:, :, None] == vocab_iota).astype(jnp.bfloat16)
    local_embed = jnp.einsum(
        "rpv,vd->rpd", local_onehot, lookup, preferred_element_type=jnp.float32
    )
    fine_input = local_embed + patch_out[0][:, None, :]
    tile_len = math.gcd(own_rows * patch_len, 128)
    tile_count = own_rows * patch_len // tile_len
    fine_input = fine_input.reshape(tile_count, tile_len, width)
    positions = jnp.arange(tile_len, dtype=jnp.int32)
    allowed_byte = (
        (positions[:, None] >= positions[None, :])
        & (positions[:, None] // patch_len == positions[None, :] // patch_len)
    )[None]

    def attend_byte(queries, keyset, valueset):
        return attention(queries, keyset, valueset, allowed_byte)

    def attend_byte_back(queries, keyset, valueset, kept, d_mixture):
        return attention_back(queries, keyset, valueset, allowed_byte, kept, d_mixture)

    byte_out, byte_saved = block_forward(fine_input, byte_weights, attend_byte)
    out_bytes = byte_out.reshape(own_rows, patch_len, width).astype(jnp.bfloat16)
    d_fine, byte_grads = block_backward(
        d_output.astype(jnp.float32).reshape(tile_count, tile_len, width),
        byte_weights,
        byte_saved,
        attend_byte_back,
    )
    d_fine = d_fine.reshape(own_rows, patch_len, width)
    d_patch = jnp.sum(d_fine, axis=1)[None]
    d_start, patch_grads = block_backward(d_patch, patch_weights, patch_saved, attend_patch_back)
    embed_local = jnp.einsum(
        "rpv,rpd->vd", local_onehot.astype(jnp.float32), d_fine, precision=lax.Precision.HIGHEST
    )
    portion = lax.all_gather(d_start[0].astype(jnp.bfloat16), SLOT, axis=0, tiled=True)
    rows_embed = slot_embed
    rows_hot = slot_onehot.astype(jnp.float32)
    proj_sum = jnp.einsum("cpd,ce->pde", rows_embed, portion, preferred_element_type=jnp.float32)
    d_rows = jnp.einsum("ce,pde->cpd", portion, project, preferred_element_type=jnp.float32)
    table_sum = jnp.einsum("cpv,cpd->vd", rows_hot, d_rows, precision=lax.Precision.HIGHEST)
    table_grad = embed_local + table_sum
    patch_pre, patch_qkv_grad, patch_mix, patch_mid, patch_exp, patch_red = patch_grads
    byte_pre, byte_qkv_grad, byte_mix, byte_mid, byte_exp, byte_red = byte_grads
    reduced = (
        lax.psum_scatter(table_grad, DP, scatter_dimension=0, tiled=True),
        lax.psum_scatter(patch_pre, DP, scatter_dimension=0, tiled=True),
        lax.psum_scatter(patch_qkv_grad, DP, scatter_dimension=0, tiled=True),
        lax.psum_scatter(patch_mix, DP, scatter_dimension=0, tiled=True),
        lax.psum_scatter(patch_mid, DP, scatter_dimension=0, tiled=True),
        lax.psum_scatter(patch_exp, DP, scatter_dimension=0, tiled=True),
        lax.psum_scatter(patch_red, DP, scatter_dimension=0, tiled=True),
        lax.psum_scatter(byte_pre, DP, scatter_dimension=0, tiled=True),
        lax.psum_scatter(byte_qkv_grad, DP, scatter_dimension=0, tiled=True),
        lax.psum_scatter(byte_mix, DP, scatter_dimension=0, tiled=True),
        lax.psum_scatter(byte_mid, DP, scatter_dimension=0, tiled=True),
        lax.psum_scatter(byte_exp, DP, scatter_dimension=0, tiled=True),
        lax.psum_scatter(byte_red, DP, scatter_dimension=0, tiled=True),
        lax.psum_scatter(proj_sum, DP, scatter_dimension=1, tiled=True),
    )
    shares = (
        lax.psum_scatter(
            reduced[0].astype(jnp.bfloat16), SLOT, scatter_dimension=0, tiled=True
        ).astype(jnp.float32),
        lax.psum_scatter(
            reduced[1].astype(jnp.bfloat16), SLOT, scatter_dimension=0, tiled=True
        ).astype(jnp.float32),
        lax.psum_scatter(
            reduced[2].astype(jnp.bfloat16), SLOT, scatter_dimension=0, tiled=True
        ).astype(jnp.float32),
        lax.psum_scatter(
            reduced[3].astype(jnp.bfloat16), SLOT, scatter_dimension=0, tiled=True
        ).astype(jnp.float32),
        lax.psum_scatter(
            reduced[4].astype(jnp.bfloat16), SLOT, scatter_dimension=0, tiled=True
        ).astype(jnp.float32),
        lax.psum_scatter(
            reduced[5].astype(jnp.bfloat16), SLOT, scatter_dimension=0, tiled=True
        ).astype(jnp.float32),
        lax.psum_scatter(
            reduced[6].astype(jnp.bfloat16), SLOT, scatter_dimension=0, tiled=True
        ).astype(jnp.float32),
        lax.psum_scatter(
            reduced[7].astype(jnp.bfloat16), SLOT, scatter_dimension=0, tiled=True
        ).astype(jnp.float32),
        lax.psum_scatter(
            reduced[8].astype(jnp.bfloat16), SLOT, scatter_dimension=0, tiled=True
        ).astype(jnp.float32),
        lax.psum_scatter(
            reduced[9].astype(jnp.bfloat16), SLOT, scatter_dimension=0, tiled=True
        ).astype(jnp.float32),
        lax.psum_scatter(
            reduced[10].astype(jnp.bfloat16), SLOT, scatter_dimension=0, tiled=True
        ).astype(jnp.float32),
        lax.psum_scatter(
            reduced[11].astype(jnp.bfloat16), SLOT, scatter_dimension=0, tiled=True
        ).astype(jnp.float32),
        lax.psum_scatter(
            reduced[12].astype(jnp.bfloat16), SLOT, scatter_dimension=0, tiled=True
        ).astype(jnp.float32),
    )
    summed = (
        lax.all_gather(shares[0].astype(jnp.bfloat16), SLOT, axis=0, tiled=True).astype(
            jnp.float32
        ),
        lax.all_gather(shares[1].astype(jnp.bfloat16), SLOT, axis=0, tiled=True).astype(
            jnp.float32
        ),
        lax.all_gather(shares[2].astype(jnp.bfloat16), SLOT, axis=0, tiled=True).astype(
            jnp.float32
        ),
        lax.all_gather(shares[3].astype(jnp.bfloat16), SLOT, axis=0, tiled=True).astype(
            jnp.float32
        ),
        lax.all_gather(shares[4].astype(jnp.bfloat16), SLOT, axis=0, tiled=True).astype(
            jnp.float32
        ),
        lax.all_gather(shares[5].astype(jnp.bfloat16), SLOT, axis=0, tiled=True).astype(
            jnp.float32
        ),
        lax.all_gather(shares[6].astype(jnp.bfloat16), SLOT, axis=0, tiled=True).astype(
            jnp.float32
        ),
        lax.all_gather(shares[7].astype(jnp.bfloat16), SLOT, axis=0, tiled=True).astype(
            jnp.float32
        ),
        lax.all_gather(shares[8].astype(jnp.bfloat16), SLOT, axis=0, tiled=True).astype(
            jnp.float32
        ),
        lax.all_gather(shares[9].astype(jnp.bfloat16), SLOT, axis=0, tiled=True).astype(
            jnp.float32
        ),
        lax.all_gather(shares[10].astype(jnp.bfloat16), SLOT, axis=0, tiled=True).astype(
            jnp.float32
        ),
        lax.all_gather(shares[11].astype(jnp.bfloat16), SLOT, axis=0, tiled=True).astype(
            jnp.float32
        ),
        lax.all_gather(shares[12].astype(jnp.bfloat16), SLOT, axis=0, tiled=True).astype(
            jnp.float32
        ),
    )
    proj_final = reduced[13]
    return (
        out_bytes,
        summed[0],
        proj_final,
        summed[1],
        summed[2],
        summed[3],
        summed[4],
        summed[5],
        summed[6],
        summed[7],
        summed[8],
        summed[9],
        summed[10],
        summed[11],
        summed[12],
    )


def generic_solution(mesh):
    placed = (
        P(DP, None),
        P(DP, None),
        P(DP, None),
        P(SLOT, DP, None),
        P(DP),
        P(DP, None),
        P(DP, None),
        P(DP),
        P(DP, None),
        P(DP, None),
        P(DP),
        P(DP, None),
        P(DP, None),
        P(DP),
        P(DP, None),
        P(DP, None),
        P((DP, SLOT), None, None),
    )
    return jax.shard_map(
        generic_local,
        mesh=mesh,
        in_specs=placed,
        out_specs=(
            P((DP, SLOT), None, None),
            P(DP, None),
            P(SLOT, DP, None),
            P(DP),
            P(DP, None),
            P(DP, None),
            P(DP),
            P(DP, None),
            P(DP, None),
            P(DP),
            P(DP, None),
            P(DP, None),
            P(DP),
            P(DP, None),
            P(DP, None),
        ),
        check_vma=False,
    )


W, SP = 4, 2
XD = 3 * SP
YD = XD + SP


class Gather:
    def __init__(self, chunks, sems):
        self.ch = chunks
        self.s = sems
        dp = lax.axis_index(DP); slot = lax.axis_index(SLOT)
        self.dp, self.slot = dp, slot
        self.z, self.x = dp // 2, dp % 2
        self.y, self.c = slot // 2, slot % 2
        self.xdev = (self.z * 2 + 1 - self.x, slot)
        self.ydev = (dp, (1 - self.y) * 2 + self.c)
        self.cdev = (dp, self.y * 2 + 1 - self.c)
        self.sent = []
    def zdev(self, d): return ((self.z + d) * 2 + self.x, self.slot)
    def barrier_peers(self):
        z = self.z
        return [(None, self.xdev), (None, self.ydev), (None, self.cdev), (z > 0, self.zdev(-1)), (z < 3, self.zdev(1))]
    def cp(self, src, dst, ss, rs, dev):
        return pltpu.make_async_remote_copy(src_ref=src, dst_ref=dst, send_sem=ss, recv_sem=rs, device_id=dev, device_id_type=MESH)
    def send(self, pred, *a):
        if pred is None: self.cp(*a).start()
        else:
            @pl.when(pred)
            def _(): self.cp(*a).start()
    def reg(self, t, oz, ox, y, c):
        k = self.ch[t]
        return k.dst(oz, ox, y, c)
    def start(self, t):
        k = self.ch[t]; z, x, y, c = self.z, self.x, self.y, self.c
        zs, zr, xs, xr = self.s.zs, self.s.zr, self.s.xs, self.s.xr
        src = k.src(y, c); dst = self.reg(t, z, x, y, c)
        one = k.kind == SINGLE
        mine = z == self.slot
        self.send((z < 3) & mine if one else z < 3, src, dst, zs.at[t, 0, z], zr.at[t, z], self.zdev(1))
        self.send((z > 0) & mine if one else z > 0, src, dst, zs.at[t, 1, z], zr.at[t, z], self.zdev(-1))
        if k.kind != ZONLY:
            self.send(mine if one else None, src, dst, xs.at[t, 0], xr.at[t, 0], self.xdev)
    def wait(self, ref, rs, ss):
        self.cp(ref, ref, ss, rs, (self.dp, self.slot)).wait_recv()
    def zarr(self, t, d):
        k = self.ch[t]; z, x, y, c = self.z, self.x, self.y, self.c; S = self.s
        for side in (-1, 1):
            oz = z + side * d
            ok = oz == self.slot if k.kind == SINGLE else (oz >= 0) & (oz <= 3)
            nxt = -side
            nok = (z + nxt >= 0) & (z + nxt <= 3)
            @pl.when(ok)
            def _():
                r = self.reg(t, oz, x, y, c)
                self.wait(r, S.zr.at[t, oz], S.zs.at[t, 0, z])
                if d < 3:
                    @pl.when(nok)
                    def _(): self.cp(r, r, S.zs.at[t, 0 if nxt == 1 else 1, oz], S.zr.at[t, oz], self.zdev(nxt)).start()
                if k.kind != ZONLY:
                    self.cp(r, r, S.xs.at[t, 0], S.xr.at[t, 0], self.xdev).start()
                if k.kind == SHARED:
                    q = k.pos
                    self.cp(r, r, S.ys.at[q, 0], S.yr.at[q, 0], self.ydev).start()
    def xarr(self, t):
        k = self.ch[t]; x, y, c = self.x, self.y, self.c; S = self.s
        if k.kind == ZONLY: return
        r = k.xall(1 - x, y, c)
        self.wait(r, S.xr.at[t, 0], S.xs.at[t, 0])
        if k.kind == SHARED:
            q = k.pos
            self.cp(r, r, S.ys.at[q, 1], S.yr.at[q, 1], self.ydev).start()
            r = k.all(y, c)
            self.cp(r, r, S.cs.at[q, 0], S.cr.at[q, 0], self.cdev).start()
    def yarr(self, t):
        k = self.ch[t]; x, y, c = self.x, self.y, self.c; S = self.s
        if k.kind != SHARED: return
        q = k.pos
        self.wait(k.three(1 - y, c), S.yr.at[q, 0], S.ys.at[q, 0])
        self.wait(k.xall(1 - x, 1 - y, c), S.yr.at[q, 1], S.ys.at[q, 1])
        r = k.all(1 - y, c)
        self.cp(r, r, S.cs.at[q, 1], S.cr.at[q, 1], self.cdev).start()
    def finish(self, t):
        k = self.ch[t]; y, c = self.y, self.c; S = self.s
        if k.kind != SHARED: return
        q = k.pos
        for h in (0, 1):
            self.wait(k.all(y if h == 0 else 1 - y, 1 - c), S.cr.at[q, h], S.cs.at[q, h])
    def drain(self, t):
        k = self.ch[t]; z, x, y, c = self.z, self.x, self.y, self.c; S = self.s
        r = self.reg(t, z, x, y, c)
        def ws(ss, r): self.cp(r, r, ss, ss, (self.dp, self.slot)).wait_send()
        if k.kind == SINGLE:
            @pl.when((z < 3) & (self.slot <= z))
            def _(): ws(S.zs.at[t, 0, self.slot], r)
            @pl.when((z > 0) & (self.slot >= z))
            def _(): ws(S.zs.at[t, 1, self.slot], r)
        else:
            for i in range(4):
                @pl.when((z < 3) & (i <= z))
                def _(): ws(S.zs.at[t, 0, i], r)
                @pl.when((z > 0) & (i >= z))
                def _(): ws(S.zs.at[t, 1, i], r)
        if k.kind != ZONLY: ws(S.xs.at[t, 0], k.xall(x, y, c))
        if k.kind == SHARED:
            q = k.pos
            ws(S.ys.at[q, 0], k.three(y, c)); ws(S.ys.at[q, 1], k.xall(1 - x, y, c))
            for h in (0, 1): ws(S.cs.at[q, h], k.all(y, c))
    def steps(self):
        n = len(self.ch)
        for t in range(min(W, n)): self.start(t)
        yield
        for i in range(n + YD):
            for d in (1, 2, 3):
                t = i - SP * (d - 1)
                if 0 <= t < n: self.zarr(t, d)
            if i + W < n: self.start(i + W)
            t = i - XD
            if 0 <= t < n: self.xarr(t)
            t = i - YD
            if 0 <= t < n: self.yarr(t)
            yield
        for t in range(n): self.finish(t)
        yield
        for t in range(n): self.drain(t)


def gather_sems(plan, count):
    T = len(plan)
    Q = max(1, sum(p[1] == SHARED for p in plan))
    D = pltpu.SemaphoreType.DMA
    return [D((T, 2, 4)), D((T, 4)), D((T, 1)), D((T, 1)), D((Q, 2)), D((Q, 2)), D((Q, 2)), D((Q, 2)), D((count,))]


def gather_chunks(plan, ins, outs):
    chunks = []
    pos = 0
    for (a, kind, j, c0, cw) in plan:
        i, o = ins[a], outs[a]
        if kind == SHARED:
            col = pl.ds(c0, cw)
            src = lambda y, c, i=i, j=j, col=col: i.at[j, y, c, :, col]
            dst = lambda oz, ox, y, c, o=o, j=j, col=col: o.at[oz, ox, j, y, c, :, col]
            xall = lambda ox, y, c, o=o, j=j, col=col: o.at[:, ox, j, y, c, :, col]
            al = lambda y, c, o=o, j=j, col=col: o.at[:, :, j, y, c, :, col]
            three = lambda y, c, o=o, j=j, col=col: o.at[pl.ds(0, 3), 0, j, y, c, :, col]
            chunks.append(NS(kind=kind, src=src, dst=dst, pos=pos, xall=xall, all=al, three=three))
            pos += 1
            continue
        src = lambda y, c, i=i, j=j: i.at[j]
        if kind == PRIVATE:
            dst = lambda oz, ox, y, c, o=o, j=j: o.at[j, oz, ox]
            xall = lambda ox, y, c, o=o, j=j: o.at[j, :, ox]
        elif kind == ZONLY:
            dst = lambda oz, ox, y, c, o=o, j=j: o.at[j, oz]
            xall = None
        else:
            dst = lambda oz, ox, y, c, o=o, j=j: o.at[j, ox]
            xall = lambda ox, y, c, o=o, j=j: o.at[j, ox]
        chunks.append(NS(kind=kind, src=src, dst=dst, xall=xall))
    return chunks


def gather_kernel(plan, nin, *refs):
    ins = refs[:nin]
    outs = refs[nin : 2 * nin]
    bounce = refs[2 * nin : 3 * nin]
    zs, zr, xs, xr, ys, yr, cs, cr, ls = refs[3 * nin :]
    sems = NS(zs=zs, zr=zr, xs=xs, xr=xr, ys=ys, yr=yr, cs=cs, cr=cr, ls=ls)
    g = Gather(gather_chunks(plan, ins, outs), sems)
    bar = pltpu.get_barrier_semaphore()
    for pred, dev in g.barrier_peers():
        def sig(dev=dev): pl.semaphore_signal(bar, inc=1, device_id=dev, device_id_type=MESH)
        if pred is None: sig()
        else: pl.when(pred)(sig)
    inner = (g.z > 0) & (g.z < 3)
    @pl.when(inner)
    def _(): pl.semaphore_wait(bar, 5)
    @pl.when(jnp.logical_not(inner))
    def _(): pl.semaphore_wait(bar, 4)
    st = g.steps()
    next(st)
    kinds = {p[0]: p[1] for p in plan}
    def inside(a):
        i = ins[a].at[:, :, g.c] if kinds[a] == SHARED else ins[a]
        return pltpu.make_async_copy(i, bounce[a], sems.ls.at[a])
    def outside(a):
        o, kind = outs[a], kinds[a]
        if kind == SHARED: o = o.at[g.z, g.x, :, :, g.c]
        elif kind == PRIVATE: o = o.at[:, g.z, g.x]
        elif kind == ZONLY: o = o.at[:, g.z]
        else: o = o.at[:, g.x]
        return pltpu.make_async_copy(bounce[a], o, sems.ls.at[a])
    def each(fn):
        for a in range(nin):
            if kinds[a] == SINGLE:
                @pl.when(g.z == g.slot)
                def _(): fn(a)
            else: fn(a)
    each(lambda a: inside(a).start())
    def turn(a):
        inside(a).wait()
        outside(a).start()
    each(turn)
    next(st)
    each(lambda a: outside(a).wait())
    for _ in st: pass


def gather_all(arrs, kinds, plan, cid, name):
    outs = []
    bounce = []
    for a, k in zip(arrs, kinds):
        bounce.append(pltpu.VMEM(a.shape[:2] + a.shape[3:] if k == SHARED else a.shape, a.dtype))
        if k == SHARED: s = (4, 2) + a.shape
        elif k == PRIVATE: s = (a.shape[0], 4, 2) + a.shape[1:]
        elif k == ZONLY: s = (a.shape[0], 4) + a.shape[1:]
        else: s = (a.shape[0], 2) + a.shape[1:]
        outs.append(jax.ShapeDtypeStruct(s, a.dtype))
    hbm = pl.BlockSpec(memory_space=pl.ANY)
    return pl.pallas_call(
        functools.partial(gather_kernel, plan, len(arrs)),
        out_shape=outs,
        in_specs=[hbm] * len(arrs),
        out_specs=[hbm] * len(outs),
        scratch_shapes=bounce + gather_sems(plan, len(arrs)),
        compiler_params=pltpu.CompilerParams(collective_id=cid, has_side_effects=True, vmem_limit_bytes=40 * 2**20),
        name=name,
    )(*arrs)


DIM = 768
SPR = 2


class Reduce:
    def __init__(self, chunks):
        self.ch = chunks
        dp = lax.axis_index(DP); slot = lax.axis_index(SLOT)
        self.dp, self.slot = dp, slot
        self.z, self.x = dp // 2, dp % 2
        self.y, self.c = slot // 2, slot % 2
        self.xdev = (self.z * 2 + 1 - self.x, slot)
        self.ydev = (dp, (1 - self.y) * 2 + self.c)
        self.cdev = (dp, self.y * 2 + 1 - self.c)
        self.ycdev = (dp, (1 - self.y) * 2 + 1 - self.c)
    def zdev(self, k): return (((self.z + k) % 4) * 2 + self.x, self.slot)
    def peers(self): return [self.xdev, self.ydev, self.cdev, self.ycdev, self.zdev(1), self.zdev(2), self.zdev(3)]
    def cp(self, src, dst, sems, i, dev):
        return pltpu.make_async_remote_copy(src_ref=src, dst_ref=dst, send_sem=sems[0].at[i], recv_sem=sems[1].at[i], device_id=dev, device_id_type=MESH)
    def ccopy(self, k): return self.cp(k.g(1 - self.c), k.rc, k.sem, 0, self.cdev)
    def load(self, k): return pltpu.make_async_copy(k.g(self.c) if k.kind == SHARED else k.g, k.own, k.lsem.at[0])
    def ycopy(self, k): return self.cp(k.own.at[:, :, 1 - self.y], k.ry, k.sem, 1, self.ydev)
    def cur(self, k, oz, ox):
        return k.own.at[oz, ox, self.y] if k.kind == SHARED else k.own.at[oz, ox]
    def xcopy(self, k):
        src = k.own.at[:, 1 - self.x, self.y] if k.kind == SHARED else k.own.at[:, 1 - self.x]
        return self.cp(src, k.rx, k.sem, 2, self.xdev)
    def zcopy(self, k, d):
        return self.cp(self.cur(k, (self.z + d) % 4, self.x), k.rz.at[d - 1], k.sem, 2 + d, self.zdev(d))
    def fcopy(self, k, i):
        y, c = self.y, self.c
        if i == 0: return self.cp(k.fin, k.out(y, c), k.sem, 6, self.ydev)
        if i == 1: return self.cp(k.fin, k.out(y, c), k.sem, 7, self.cdev)
        return self.cp(k.out(1 - y, c), k.out(1 - y, c), k.sem, 8, self.cdev)
    def put(self, k): return pltpu.make_async_copy(k.fin, k.out(self.y, self.c), k.lsem.at[1])
    def s0(self, k):
        self.load(k).start()
        if k.kind == SHARED: self.ccopy(k).start()
    def s1(self, k):
        self.load(k).wait()
        if k.kind != SHARED: return
        self.ccopy(k).wait_recv()
        own, rc = k.own, k.rc
        @pl.loop(0, 4)
        def _(i):
            own[i] = own[i] + rc[i]
        self.ycopy(k).start()
    def s2(self, k):
        if k.kind == SHARED:
            self.ycopy(k).wait_recv()
            own, ry = k.own, k.ry
            @pl.loop(0, 4)
            def _(i):
                own[i, :, self.y] = own[i, :, self.y] + ry[i]
        self.xcopy(k).start()
    def s3(self, k):
        self.xcopy(k).wait_recv()
        rx = k.rx
        @pl.loop(0, 4)
        def _(i):
            r = self.cur(k, i, self.x)
            r[...] = r[...] + rx[i]
        for d in (1, 3, 2): self.zcopy(k, d).start()
    def s4(self, k):
        for d in (1, 3, 2): self.zcopy(k, d).wait_recv()
        rz = k.rz; f = jnp.float32
        k.fin[...] = (self.cur(k, self.z, self.x)[...].astype(f) + rz[0].astype(f) + rz[1].astype(f) + rz[2].astype(f)).astype(jnp.bfloat16)
        self.put(k).start()
        self.fcopy(k, 0).start(); self.fcopy(k, 1).start()
    def s5(self, k):
        self.fcopy(k, 0).wait_recv()
        self.fcopy(k, 2).start()
    def s6(self, k):
        self.fcopy(k, 1).wait_recv(); self.fcopy(k, 2).wait_recv()
        if k.kind == SHARED: self.ccopy(k).wait_send(); self.ycopy(k).wait_send()
        self.xcopy(k).wait_send()
        for d in (1, 2, 3): self.zcopy(k, d).wait_send()
        for i in range(3): self.fcopy(k, i).wait_send()
        self.put(k).wait()
    def steps(self):
        n = len(self.ch)
        for k in self.ch: self.s0(k)
        yield
        st = [self.s1, self.s2, self.s3, self.s4, self.s5]
        for i in range(n + SPR * 4):
            for q, fn in enumerate(st):
                t = i - SPR * q
                if 0 <= t < n: fn(self.ch[t])
            yield
        for k in self.ch: self.s6(k)

class Mixer:
    def __init__(self, r, g, own, rx, rz, fin, out, ss, rs, ls):
        self.r, self.g, self.own, self.rx, self.rz, self.fin, self.out, self.ss, self.rs, self.ls = r, g, own, rx, rz, fin, out, ss, rs, ls
    def xc(self):
        r = self.r
        return r.cp(self.own.at[1 - r.x], self.rx, (self.ss, self.rs), 0, r.xdev)
    def zc(self, d):
        r = self.r
        return r.cp(self.own.at[r.x], self.rz.at[d - 1], (self.ss, self.rs), d, (r.slot * 2 + r.x, r.slot))
    def bc(self, i):
        r = self.r
        return r.cp(self.fin, self.out, (self.ss, self.rs), 4 + i, (r.ydev, r.cdev, r.ycdev)[i])
    def steps(self):
        r = self.r
        ld = pltpu.make_async_copy(self.g, self.own, self.ls.at[0])
        ld.start(); ld.wait()
        self.xc().start(); yield
        self.xc().wait_recv()
        self.own[r.x] = self.own[r.x] + self.rx[...]
        for d in (1, 2, 3):
            @pl.when((r.z + d) % 4 == r.slot)
            def _(): self.zc(d).start()
        yield; yield; yield
        put = pltpu.make_async_copy(self.fin, self.out, self.ls.at[1])
        @pl.when(r.z == r.slot)
        def _():
            f = jnp.float32
            for d in (1, 2, 3): self.zc(d).wait_recv()
            self.fin[...] = (self.own[r.x].astype(f) + self.rz[0].astype(f) + self.rz[1].astype(f) + self.rz[2].astype(f)).astype(jnp.bfloat16)
            put.start()
            for i in range(3): self.bc(i).start()
        yield; yield
        self.xc().wait_send()
        for d in (1, 2, 3):
            @pl.when((r.z + d) % 4 == r.slot)
            def _(): self.zc(d).wait_send()
        @pl.when(r.z == r.slot)
        def _():
            for i in range(3): self.bc(i).wait_send()
            put.wait()
        for i, s in enumerate((r.ydev[1], r.cdev[1], r.ycdev[1])):
            @pl.when(r.z == s)
            def _(): self.bc(i).wait_recv()

def reduce_kernel(plan, nin, *refs):
    ins = refs[:nin]; outs = refs[nin:2 * nin]; rest = list(refs[2 * nin:])
    ns = sum(p[1] == SHARED for p in plan); npv = len(plan) - ns
    take = lambda: rest.pop(0)
    s_own, s_rc, s_ry, s_rx, s_rz, s_fin = (take() for _ in range(6))
    pv = [[take() for _ in range(4)] for _ in range(npv)]
    m_own, m_rx, m_rz, m_fin = (take() for _ in range(4))
    ss, rs, ls, mss, mrs, mls = (take() for _ in range(6))
    chunks = []; a = b = 0
    for t, (i, kind, j, cb) in enumerate(plan):
        g, o = ins[i], outs[i]
        if kind == SHARED:
            col = pl.ds(cb * DIM, DIM)
            chunks.append(NS(kind=kind, g=lambda c, g=g, j=j, col=col: g.at[:, :, j, :, c, :, col], out=lambda y, c, o=o, j=j, col=col: o.at[j, y, c, :, col],
                               own=s_own.at[a], rc=s_rc.at[a], ry=s_ry.at[a], rx=s_rx.at[a], rz=s_rz.at[a], fin=s_fin.at[a]))
            a += 1
        else:
            p = pv[b]; b += 1
            chunks.append(NS(kind=kind, g=g.at[j], out=lambda y, c, o=o, j=j: o.at[j, y, c], own=p[0], rx=p[1], rz=p[2], fin=p[3]))
        chunks[-1].sem = (ss.at[t], rs.at[t]); chunks[-1].lsem = ls.at[t]
    r = Reduce(chunks)
    bar = pltpu.get_barrier_semaphore()
    for dev in r.peers(): pl.semaphore_signal(bar, inc=1, device_id=dev, device_id_type=MESH)
    pl.semaphore_wait(bar, 7)
    m = Mixer(r, ins[-1], m_own, m_rx, m_rz, m_fin, outs[-1], mss, mrs, mls)
    g1, g2 = r.steps(), m.steps()
    while True:
        e1 = next(g1, 0); e2 = next(g2, 0)
        if e1 == 0 and e2 == 0: break

def reduce_all(arrs, kinds, plan, mixer):
    outs = []
    for a, k in zip(arrs, kinds):
        outs.append(jax.ShapeDtypeStruct(a.shape[2:] if k == SHARED else (a.shape[0], 2, 2) + a.shape[3:], a.dtype))
    outs.append(jax.ShapeDtypeStruct(mixer.shape[1:], mixer.dtype))
    D = pltpu.SemaphoreType.DMA
    B = jnp.bfloat16
    ns = sum(p[1] == SHARED for p in plan)
    u = 24
    V = lambda *s: pltpu.VMEM(s, B)
    scr = [V(ns, 4, 2, 2, u, DIM), V(ns, 4, 2, 2, u, DIM), V(ns, 4, 2, u, DIM), V(ns, 4, u, DIM), V(ns, 3, u, DIM), V(ns, u, DIM)]
    for (i, k, j, cb) in plan:
        if k != SHARED:
            r, C = arrs[i].shape[3:]
            scr += [V(4, 2, r, C), V(4, r, C), V(3, r, C), V(r, C)]
    r, C = mixer.shape[1:]
    scr += [V(2, r, C), V(r, C), V(3, r, C), V(r, C)]
    T = len(plan)
    scr += [D((T, 9)), D((T, 9)), D((T, 2)), D((7,)), D((7,)), D((2,))]
    al = list(arrs) + [mixer]
    return pl.pallas_call(
        functools.partial(reduce_kernel, plan, len(al)), out_shape=outs,
        in_specs=[pl.BlockSpec(memory_space=pl.ANY)] * len(al),
        out_specs=[pl.BlockSpec(memory_space=pl.ANY)] * len(outs),
        scratch_shapes=scr,
        compiler_params=pltpu.CompilerParams(collective_id=1, has_side_effects=True, vmem_limit_bytes=60 * 2**20),
        name="reduce_grads",
    )(*al)


def sum_kernel(with_x, p_ref, o_ref, rx, s0, rc, s1, ry, fin, rf, ss, rs):
    dp = lax.axis_index(DP)
    slot = lax.axis_index(SLOT)
    z, x, y, c = dp // 2, dp % 2, slot // 2, slot % 2
    xdev = (z * 2 + 1 - x, slot)
    ydev = (dp, (1 - y) * 2 + c)
    cdev = (dp, y * 2 + 1 - c)
    peers = [ydev, cdev] + ([xdev] if with_x else [])
    bar = pltpu.get_barrier_semaphore()
    for d in peers:
        pl.semaphore_signal(bar, inc=1, device_id=d, device_id_type=MESH)
    pl.semaphore_wait(bar, len(peers))

    def rc_(src, dst, i, dev):
        return pltpu.make_async_remote_copy(src_ref=src, dst_ref=dst, send_sem=ss.at[i], recv_sem=rs.at[i], device_id=dev, device_id_type=MESH)

    cps = []
    if with_x:
        a = rc_(p_ref.at[1 - x], rx, 0, xdev)
        a.start()
        a.wait_recv()
        cps.append(a)
        s0[...] = (p_ref[x].astype(F32) + rx[...].astype(F32)).astype(BF)
        base = s0
    else:
        base = p_ref
    b = rc_(base.at[1 - c], rc, 1, cdev)
    b.start()
    b.wait_recv()
    s1[...] = (base[c].astype(F32) + rc[...].astype(F32)).astype(BF)
    d = rc_(s1, ry, 2, ydev)
    d.start()
    d.wait_recv()
    total = (s1[...].astype(F32) + ry[...].astype(F32)).astype(BF)
    fin[...] = total
    e = rc_(fin, rf, 3, cdev)
    e.start()
    o_ref[c] = total.astype(F32)
    e.wait_recv()
    o_ref[1 - c] = rf[...].astype(F32)
    for k in cps + [b, d, e]:
        k.wait_send()


def slot_sum(part, cid, with_x=False):
    rows, width = part.shape[-2] // 2, part.shape[-1]
    shape = part.shape[:-2] + (2, rows, width)
    V = lambda *s: pltpu.VMEM(s, BF)
    D = pltpu.SemaphoreType.DMA
    vm = pl.BlockSpec(memory_space=pltpu.VMEM)
    out = pl.pallas_call(
        functools.partial(sum_kernel, with_x),
        out_shape=jax.ShapeDtypeStruct((2, rows, width), F32),
        in_specs=[vm],
        out_specs=vm,
        scratch_shapes=[V(2, rows, width), V(2, rows, width)] + [V(rows, width)] * 5 + [D((4,)), D((4,))],
        compiler_params=pltpu.CompilerParams(collective_id=cid, has_side_effects=True),
        name="slot_sum",
    )(part.reshape(shape))
    return out.reshape(2 * rows, width)


def slot_gather_kernel(p_ref, o_ref, sy, ss, rs):
    dp = lax.axis_index(DP)
    slot = lax.axis_index(SLOT)
    y, c = slot // 2, slot % 2
    ydev = (dp, (1 - y) * 2 + c)
    cdev = (dp, y * 2 + 1 - c)
    bar = pltpu.get_barrier_semaphore()
    for d in (ydev, cdev):
        pl.semaphore_signal(bar, inc=1, device_id=d, device_id_type=MESH)
    pl.semaphore_wait(bar, 2)

    def rc_(src, dst, i, dev):
        return pltpu.make_async_remote_copy(src_ref=src, dst_ref=dst, send_sem=ss.at[i], recv_sem=rs.at[i], device_id=dev, device_id_type=MESH)

    a = rc_(p_ref, o_ref.at[slot], 0, ydev)
    b = rc_(p_ref, o_ref.at[slot], 1, cdev)
    a.start()
    b.start()
    o_ref[slot] = p_ref[...]
    theirs = o_ref.at[ydev[1]]
    a.wait_recv()
    e = rc_(theirs, theirs, 2, cdev)
    e.start()
    b.wait_recv()
    e.wait_recv()
    for k in (a, b, e):
        k.wait_send()


def slot_gather(part, cid):
    D = pltpu.SemaphoreType.DMA
    vm = pl.BlockSpec(memory_space=pltpu.VMEM)
    out = pl.pallas_call(
        slot_gather_kernel,
        out_shape=jax.ShapeDtypeStruct((4,) + part.shape, part.dtype),
        in_specs=[vm],
        out_specs=vm,
        scratch_shapes=[pltpu.VMEM((8, 128), BF), D((3,)), D((3,))],
        compiler_params=pltpu.CompilerParams(collective_id=cid, has_side_effects=True),
        name="slot_gather",
    )(part)
    return out.reshape(4 * part.shape[0], part.shape[1])


def mm(spec, a, b):
    return jnp.einsum(spec, a, b, preferred_element_type=F32)


def local(
    byte_ids,
    seg_ids,
    embed_table,
    slot_project,
    patch_prenorm,
    patch_heads,
    patch_mixer,
    patch_midnorm,
    patch_expand,
    patch_reduce,
    byte_prenorm,
    byte_heads,
    byte_mixer,
    byte_midnorm,
    byte_expand,
    byte_reduce,
    d_output,
):
    dp = lax.axis_index(DP)
    slot = lax.axis_index(SLOT)
    x = dp % 2
    group_rows, patch_len = byte_ids.shape
    own_rows = group_rows // 4
    vocab_part, width = embed_table.shape
    vocab = vocab_part * 8
    share = width // 8
    ff = patch_expand.shape[1]
    quarter = share // 4
    pick = lambda v, axis: lax.dynamic_index_in_dim(v, slot, axis, keepdims=False)
    gains = jnp.concatenate([patch_prenorm, patch_midnorm, byte_prenorm, byte_midnorm])[None]
    gains = jnp.pad(gains, ((0, share - vocab_part - 1), (0, width - 4 * share)))
    misc = jnp.concatenate([embed_table, gains], axis=0)
    heads_own = pick(patch_heads.reshape(share, 3, 4, width // 4), 2).reshape(1, share, 3 * width // 4)
    expand_own = pick(patch_expand.reshape(share, 8, 4, share), 2).reshape(1, share, width)
    reduce_own = pick(patch_reduce.reshape(4, share, width), 0)[None]
    shared = lambda v: v.reshape(v.shape[0] // share, 2, 2, quarter, v.shape[1])
    arrs = [
        shared(misc), byte_ids.T[None], slot_project, heads_own, expand_own, reduce_own, patch_mixer[None],
        shared(byte_heads), shared(byte_mixer), shared(byte_expand), shared(byte_reduce),
    ]
    kinds = [SHARED, PRIVATE, ZONLY, PRIVATE, PRIVATE, PRIVATE, SINGLE] + [SHARED] * 4
    plan = [(0, SHARED, 0, 0, width), (1, PRIVATE, 0, 0, 0)]
    plan += [(7, SHARED, 0, i * width, width) for i in range(3)] + [(8, SHARED, 0, 0, width)]
    plan += [(9, SHARED, 0, i * width, width) for i in range(4)] + [(10, SHARED, i, 0, width) for i in range(4)]
    plan += [(3, PRIVATE, 0, 0, 0), (6, SINGLE, 0, 0, 0), (4, PRIVATE, 0, 0, 0), (5, PRIVATE, 0, 0, 0)]
    plan += [(2, ZONLY, 0, 0, 0), (2, ZONLY, 1, 0, 0)]
    full = gather_all(arrs, kinds, plan, 0, "gather_weights")
    misc_all = full[0].reshape(8, share, width)
    lookup = misc_all[:, :vocab_part].reshape(vocab, width)
    gains_all = misc_all[:, vocab_part, : 4 * share].reshape(8, 4, share).transpose(1, 0, 2).reshape(4, width)
    gains_all = gains_all.astype(F32)
    ids_all = full[1].reshape(8, patch_len, group_rows)
    project = full[2].reshape(2, 4 * share, width)
    p_heads = full[3].reshape(width, 3 * width // 4)
    p_expand = full[4].reshape(width, width)
    p_reduce = full[5].reshape(width, width)
    p_mixer = full[6].reshape(width // 4, width)
    b_heads = full[7].reshape(width, 3 * width)
    b_mixer = full[8].reshape(width, width)
    b_expand = full[9].reshape(width, ff)
    b_reduce = full[10].reshape(ff, width)
    vocab_iota = jnp.arange(vocab, dtype=jnp.int32)
    hot = lambda ids: (ids[..., None] == vocab_iota).astype(BF)

    z_ids = lax.dynamic_slice_in_dim(ids_all, (dp // 2) * 2, 2, 0)
    pair_ids = lax.dynamic_slice_in_dim(z_ids, slot * 2, 2, 1)
    lookup_parts = lookup.reshape(vocab, 4, 2, share)
    lookup_x = lax.dynamic_index_in_dim(lookup_parts, x, 2, keepdims=False).reshape(vocab, 4 * share)
    pair_tokens = mm("xpgv,vf->xpgf", hot(pair_ids), lookup_x).astype(BF)
    start_part = mm("xpgf,pfe->xge", pair_tokens, project).astype(BF)
    start = slot_sum(start_part, 2, True)

    segments = seg_ids[0]
    pos = jnp.arange(group_rows, dtype=jnp.int32)
    allowed_patch = ((pos[:, None] >= pos[None, :]) & (segments[:, None] == segments[None, :]))[None]
    heads = 3 * width // 4
    head_count = width // 4 // HEAD_DIM
    norm_one, back_one = jax.vjp(norm_rows, start, gains_all[0])
    norm_one = norm_one.astype(BF)
    joined = mm("nd,df->nf", norm_one, p_heads).astype(BF).reshape(1, group_rows, 3, head_count, HEAD_DIM)
    mixture, logsum = attention(joined[:, :, 0], joined[:, :, 1], joined[:, :, 2], allowed_patch)
    mixture = mixture.astype(BF).reshape(group_rows, width // 4)
    middle = start + slot_sum(mm("nf,fd->nd", mixture, p_mixer).astype(BF), 3)
    norm_two, back_two = jax.vjp(norm_rows, middle, gains_all[1])
    norm_two = norm_two.astype(BF)
    expanded = mm("nd,df->nf", norm_two, p_expand)
    hidden, back_gelu = jax.vjp(gelu_tanh, expanded)
    hidden = hidden.astype(BF)
    patch_out = middle + slot_sum(mm("nf,fd->nd", hidden, p_reduce).astype(BF), 4)

    first_row = slot * own_rows
    own_out = lax.dynamic_slice_in_dim(patch_out, first_row, own_rows, 0)
    local_bytes = lax.dynamic_slice_in_dim(byte_ids, first_row, own_rows, 0)
    local_onehot = hot(local_bytes)
    local_embed = mm("rpv,vd->rpd", local_onehot, lookup)
    fine_input = local_embed + own_out[:, None, :]
    tile_len = math.gcd(own_rows * patch_len, 128)
    tile_count = own_rows * patch_len // tile_len
    fine_input = fine_input.reshape(tile_count, tile_len, width)
    positions = jnp.arange(tile_len, dtype=jnp.int32)
    allowed_byte = (
        (positions[:, None] >= positions[None, :])
        & (positions[:, None] // patch_len == positions[None, :] // patch_len)
    )[None]

    def attend_byte(queries, keyset, valueset):
        return attention(queries, keyset, valueset, allowed_byte)

    def attend_byte_back(queries, keyset, valueset, kept, d_mixture):
        return attention_back(queries, keyset, valueset, allowed_byte, kept, d_mixture)

    byte_weights = (gains_all[2], b_heads, b_mixer, gains_all[3], b_expand, b_reduce)
    byte_out, byte_saved = block_forward(fine_input, byte_weights, attend_byte)
    out_bytes = byte_out.reshape(own_rows, patch_len, width).astype(BF)
    d_fine, byte_grads = block_backward(
        d_output.astype(F32).reshape(tile_count, tile_len, width), byte_weights, byte_saved, attend_byte_back
    )
    d_fine = d_fine.reshape(own_rows, patch_len, width)

    g_low = slot_gather(jnp.sum(d_fine, axis=1).astype(BF), 7)
    grad = g_low.astype(F32)
    g_reduce = mm("nf,nd->fd", hidden, g_low).astype(BF)
    (d_expanded,) = back_gelu(mm("nd,fd->nf", g_low, p_reduce))
    d_expanded = d_expanded.astype(BF)
    g_expand = mm("nd,nf->df", norm_two, d_expanded).astype(BF)
    d_norm_two = slot_sum(mm("nf,df->nd", d_expanded, p_expand).astype(BF), 5)
    d_middle_part, g_midnorm = back_two(d_norm_two)
    d_middle = grad + d_middle_part
    middle_low = d_middle.astype(BF)
    g_mixer = mm("nf,nd->fd", mixture, middle_low).astype(BF)
    d_mixture = mm("nd,fd->nf", middle_low, p_mixer).astype(BF).reshape(1, group_rows, head_count, HEAD_DIM)
    d_joined = attention_back(joined[:, :, 0], joined[:, :, 1], joined[:, :, 2], allowed_patch, logsum, d_mixture)
    d_joined = jnp.stack(d_joined, axis=2).reshape(group_rows, heads).astype(BF)
    g_heads = mm("nd,nf->df", norm_one, d_joined).astype(BF)
    d_norm_one = slot_sum(mm("nf,df->nd", d_joined, p_heads).astype(BF), 6)
    d_start_part, g_prenorm = back_one(d_norm_one)
    d_start = (d_middle + d_start_part).astype(BF)

    rows_all = gather_all(
        [d_start.reshape(1, 2, 2, group_rows // 4, width)], [SHARED],
        [(0, SHARED, 0, i * (width // 3), width // 3) for i in range(3)], 8, "gather_d_start",
    )[0].reshape(8 * group_rows, width)
    slot_ids = lax.dynamic_slice_in_dim(ids_all, slot * 2, 2, 1).transpose(1, 0, 2).reshape(2, 8 * group_rows)
    by_value = mm("pgv,ge->pve", hot(slot_ids), rows_all).astype(BF)
    lookup_own = lax.dynamic_index_in_dim(lookup.reshape(vocab, 8, share), dp, 1, keepdims=False)
    project_grad = mm("vf,pve->pfe", lookup_own, by_value)
    project_wide = lax.dynamic_update_slice_in_dim(jnp.zeros((2, width, width), BF), slot_project, dp * share, 1)
    table_grad = mm("pve,pfe->vf", by_value, project_wide)
    low_fine = d_fine.astype(BF)
    rest_fine = (d_fine - low_fine.astype(F32)).astype(BF)
    table_grad = table_grad + mm("rpv,rpd->vd", local_onehot, low_fine) + mm("rpv,rpd->vd", local_onehot, rest_fine)

    first = (slot == 0).astype(F32)
    byte_pre, byte_qkv, byte_mix, byte_mid, byte_exp, byte_red = byte_grads
    gain_grads = jnp.stack([g_prenorm * first, g_midnorm * first, byte_pre, byte_mid])
    gain_grads = gain_grads.reshape(4, 8, share).transpose(1, 0, 2).reshape(8, 1, 4 * share)
    gain_grads = jnp.pad(gain_grads, ((0, 0), (0, share - vocab_part - 1), (0, width - 4 * share)))
    misc_grad = jnp.concatenate([table_grad.reshape(8, vocab_part, width), gain_grads], axis=1)
    grouped = lambda v: v.astype(BF).reshape(4, 2, v.shape[0] // width, 2, 2, quarter, v.shape[1])
    private = lambda v: v.reshape(1, 4, 2, share, v.shape[1])
    garr = [
        misc_grad.astype(BF).reshape(4, 2, 1, 2, 2, quarter, width),
        grouped(byte_qkv), grouped(byte_mix), grouped(byte_exp), grouped(byte_red),
        private(g_heads), private(g_expand), private(g_reduce),
    ]
    gkinds = [SHARED] * 5 + [PRIVATE] * 3
    bplan = [(4, SHARED, i, 0) for i in range(4)] + [(3, SHARED, 0, i) for i in range(4)]
    bplan += [(2, SHARED, 0, 0)] + [(1, SHARED, 0, i) for i in range(3)]
    gplan = bplan[:3] + [(7, PRIVATE, 0, 0)] + bplan[3:6] + [(6, PRIVATE, 0, 0)] + bplan[6:9]
    gplan += [(5, PRIVATE, 0, 0)] + bplan[9:] + [(0, SHARED, 0, 0)]
    res = reduce_all(garr, gkinds, gplan, g_mixer.reshape(2, share, width))
    misc_out = res[0].reshape(share, width).astype(F32)
    gain_out = misc_out[vocab_part, : 4 * share].reshape(4, share)
    out_heads = res[5].reshape(4, share, 3, width // 4).transpose(1, 2, 0, 3).reshape(share, 3 * width)
    out_expand = res[6].reshape(4, share, 8, share).transpose(1, 2, 0, 3).reshape(share, ff)
    return (
        out_bytes,
        misc_out[:vocab_part],
        project_grad,
        gain_out[0],
        out_heads.astype(F32),
        res[8].astype(F32),
        gain_out[1],
        out_expand.astype(F32),
        res[7].reshape(4 * share, width).astype(F32),
        gain_out[2],
        res[1].reshape(share, 3 * width).astype(F32),
        res[2].reshape(share, width).astype(F32),
        gain_out[3],
        res[3].reshape(share, ff).astype(F32),
        res[4].reshape(4 * share, width).astype(F32),
    )


def solution(mesh):
    if (mesh.shape[DP], mesh.shape[SLOT]) != (8, 4):
        return generic_solution(mesh)
    placed = (P(DP, None), P(DP, None), P(DP, None), P(SLOT, DP, None)) + (
        P(DP), P(DP, None), P(DP, None), P(DP), P(DP, None), P(DP, None),
    ) * 2 + (P((DP, SLOT), None, None),)
    outs = (P((DP, SLOT), None, None), P(DP, None), P(SLOT, DP, None)) + (
        P(DP), P(DP, None), P(DP, None), P(DP), P(DP, None), P(DP, None),
    ) * 2
    return jax.shard_map(local, mesh=mesh, in_specs=placed, out_specs=outs, check_vma=False)
```

time: 2190 us -> 474 us (0.22)
  waiting for transfers between devices: 1810 us -> 0 us
  Pallas kernels: 0 us -> 294 us
  blocking collectives: 174 us -> 0 us
  matrix products: 110 us -> 67.5 us
  local copies, waits for them, and re-layouts: 24 us -> 57.6 us
    reduce_scatter x22 -> x0, waiting for transfers between devices: 1290 us -> none  [the longest x1 165 us: local(): lax.psum_scatter(patch_exp, 'dp', scatter_dimension=0, tiled=True)]
    all_gather x9 -> x0, waiting for transfers between devices: 510 us -> none  [the longest x1 78.4 us: local(): lax.all_gather(patch_expand, 'dp', axis=0, tiled=True)]
    pallas_call x0 -> x9, Pallas kernels: none -> 294 us  [the longest x1 124 us: reduce_all(): pl.pallas_call(functools.partial(reduce_kernel, plan, len(al)), out_shape...]
    all_gather x13 -> x0, blocking collectives: 111 us -> none  [the longest x1 26.3 us: local(): lax.all_gather(embed_table, 'dp', axis=0, tiled=True)]
    unnamed x4 -> x0, blocking collectives: 63.2 us -> none
  transfers between devices with their start and end apart: 31 -> 0, of which waited for: 27 -> 0; matrix products, arithmetic and copies ran while one was open for 5% -> 0% of each run, Pallas kernels for 0% -> 0%
where the time goes in v1:
time: 474 us; the launch traced here: 465 us
  Pallas kernels  294 us (62%)
  matrix products  67.5 us (14%)
  local copies, waits for them, and re-layouts  57.6 us (12%)
  other arithmetic  43.4 us (9%)
    pallas_call x1, Pallas kernels, reduce_all(): pl.pallas_call(functools.partial(reduce_kernel, plan, len(al)), out_shape...  124 us
    pallas_call x2, Pallas kernels, gather_all(): pl.pallas_call(functools.partial(gather_kernel, plan, len(arrs)), out_sha...  112 us
    pallas_call x5, Pallas kernels, slot_sum(): pl.pallas_call(functools.partial(sum_kernel, with_x), out_shape=jax.Shape...  52 us
    dot_general x19, matrix products, mm(): return jnp.einsum(spec, a, b, preferred_element_type=F32)  22.2 us
    unnamed x239, local copies, waits for them, and re-layouts  19.9 us

profile of v1, /device:TPU:5, one launch (start us, length us, event | category | flops | bytes accessed | tf_op | source)
XLA Modules:
  0.0 465.1 jit_solution(2247054356844366808)
XLA Ops:
  2.4 1.6 reshape.1184
  16.0 92.3 %gather_weights.1 = (bf16[4,2,1,2,2,24,768]{6,5,4,3,2,1,0:T(8,128)(2,1)}, s32[1,4,2,8,128]{4,3,2,1,0:T(8,128)S(1)}, bf16[2,4,96,768]{3,2,1,0:T(8,128)(2,1)S(1)},...) custom-call(bf16[1,2,2,24,768]{4,3,2,1,0:T(8,128)(2,1)S(1)} %bitcast, ...), custom_call_target="tpu_custom_call" | custom-call | tf_op jit(solution)/shard_map/gather_weights/pallas_call | solution.py:672
  110.0 1.9 copy-done.18
  112.8 1.8 slice.87
  114.6 2.3 reshape_reshape.6
  117.0 2.4 constant_dynamic-slice_fusion.1
  119.4 2.3 copy.98
  121.7 3.0 fusion.18
  124.6 15.3 %slot_sum.5 = f32[2,64,768]{2,1,0:T(8,128)} custom-call(bf16[2,2,64,768]{3,2,1,0:T(8,128)(2,1)} %bitcast.402), custom_call_target="tpu_custom_call" | custom-call | tf_op jit(solution)/shard_map/slot_sum/pallas_call | solution.py:928
  148.4 9.3 %slot_sum.6 = f32[2,64,768]{2,1,0:T(8,128)} custom-call(bf16[2,64,768]{2,1,0:T(8,128)(2,1)} %bitcast.390), custom_call_target="tpu_custom_call" | custom-call | tf_op jit(solution)/shard_map/slot_sum/pallas_call | solution.py:928
  157.7 1.9 fusion.85
  164.1 9.3 %slot_sum.7 = f32[2,64,768]{2,1,0:T(8,128)} custom-call(bf16[2,64,768]{2,1,0:T(8,128)(2,1)} %bitcast.407), custom_call_target="tpu_custom_call" | custom-call | tf_op jit(solution)/shard_map/slot_sum/pallas_call | solution.py:928
  174.5 2.8 fusion.91
  178.1 1.3 multiply_reduce_fusion.6
  182.1 4.1 convolution_convert_fusion
  186.3 2.4 copy.101
  188.7 1.6 fusion.92
  190.6 1.7 convolution_convert_fusion.6
  192.3 1.9 fusion.93
  195.7 1.5 multiply_reduce_fusion.5
  197.8 4.1 fusion.70
  202.0 2.7 fusion.14
  204.8 3.7 fusion.4
  208.5 2.9 multiply_reduce_fusion.4
  211.5 1.4 stack.48
  212.8 1.4 add.249
  215.0 1.7 fusion.84
  219.7 2.0 copy.108
  222.6 2.2 fusion.21
  229.2 2.0 fusion.95
  231.3 1.4 multiply_reduce_fusion.3
  233.9 3.1 add_add_fusion.2
  237.0 2.0 reduce_sum.254.p_ref
  238.9 6.5 %slot_gather.1 = bf16[4,32,768]{2,1,0:T(8,128)(2,1)} custom-call(bf16[32,768]{1,0:T(8,128)(2,1)} %reduce_sum.254.p_ref), custom_call_target="tpu_custom_call" | custom-call | tf_op jit(solution)/shard_map/slot_gather/pallas_call | solution.py:972
  245.4 1.5 fusion.96
  248.4 9.1 %slot_sum.8 = f32[2,64,768]{2,1,0:T(8,128)} custom-call(bf16[2,64,768]{2,1,0:T(8,128)(2,1)} %bitcast.406), custom_call_target="tpu_custom_call" | custom-call | tf_op jit(solution)/shard_map/slot_sum/pallas_call | solution.py:928
  264.7 9.0 %slot_sum.9 = f32[2,64,768]{2,1,0:T(8,128)} custom-call(bf16[2,64,768]{2,1,0:T(8,128)(2,1)} %bitcast.391), custom_call_target="tpu_custom_call" | custom-call | tf_op jit(solution)/shard_map/slot_sum/pallas_call | solution.py:928
  276.6 1.4 convolution_bitcast_fusion.3
  279.0 19.7 %gather_d_start.1 = bf16[4,2,1,2,2,32,768]{6,5,4,3,2,1,0:T(8,128)(2,1)S(1)} custom-call(bf16[1,2,2,32,768]{4,3,2,1,0:T(8,128)(2,1)S(1)} %fusion.44.refs_0_), custom_call_target="tpu_custom_call" | custom-call | tf_op jit(solution)/shard_map/gather_d_start/pallas_call | solution.py:672
  304.8 3.0 bitcast_convert_fusion.2
  307.8 1.5 bitcast_convert_fusion.3
  309.3 3.7 bitcast_convert_fusion.1
  313.0 4.4 bitcast_convert_fusion
  319.3 1.8 convolution_convert_fusion.2
  321.1 1.6 convolution_convert_fusion.1
  323.6 123.6 %reduce_grads.1 = (bf16[1,2,2,24,768]{4,3,2,1,0:T(8,128)(2,1)}, bf16[1,2,2,24,2304]{4,3,2,1,0:T(8,128)(2,1)}, bf16[1,2,2,24,768]{4,3,2,1,0:T(8,128)(2,1)}, bf16[...) custom-call(bf16[4,2,1,2,2,24,768]{6,5,4,3,2,1,0:T(8,128)(2,1)} %bit, ...), custom_call_target="tpu_custom_call" | custom-call | tf_op jit(solution)/shard_map/reduce_grads/pallas_call | solution.py:868
  452.6 1.7 reshape.1244
  456.8 2.6 reshape.1245
  (372 shorter events, 80.1 us)
Async XLA Ops:
  0.6 7.5 %copy-start = (bf16[384,768]{1,0:T(8,128)(2,1)S(1)}, bf16[384,768]{1,0:T(8,128)(2,1)}, u32[]{:S(2)}) copy-start(bf16[384,768]{1,0:T(8,128)(2,1)} %param.26) | copy-start | bytes 1769476
  0.7 4.7 %copy-start.66 = (bf16[96,3072]{1,0:T(8,128)(2,1)S(1)}, bf16[96,3072]{1,0:T(8,128)(2,1)}, u32[]{:S(2)}) copy-start(bf16[96,3072]{1,0:T(8,128)(2,1)} %param.25) | copy-start | bytes 1769476
  4.3 3.9 copy-start.17
  142.6 4.8 %copy-start.85 = (f32[2,64]{1,0:T(2,128)}, f32[2,64]{1,0:T(2,128)S(1)}, u32[]{:S(2)}) copy-start(f32[2,64]{1,0:T(2,128)S(1)} %broadcast_multiply_fusion.3) | copy-start | bytes 1540
  144.4 3.0 copy-start.6
  146.1 115.1 %copy-start.68 = (bf16[128,576]{0,1:T(8,128)(2,1)}, bf16[128,576]{0,1:T(8,128)(2,1)S(1)}, u32[]{:S(2)}) copy-start(bf16[128,576]{0,1:T(8,128)(2,1)S(1)} %convolution_convert_fusion.13) | copy-start | bytes 442372
  147.3 12.4 %copy-start.108 = (f32[3,128]{1,0:T(4,128)}, f32[3,128]{1,0:T(4,128)S(1)}, u32[]{:S(2)}) copy-start(f32[3,128]{1,0:T(4,128)S(1)} %fusion.60) | copy-start | bytes 4612
  159.7 3.4 copy-start.3
  159.7 4.4 copy-start.83
  161.0 3.1 copy-start.97
  164.1 13.2 %copy-start.89 = (f32[8,96]{1,0:T(8,128)S(1)}, f32[8,96]{1,0:T(8,128)}, u32[]{:S(2)}) copy-start(f32[8,96]{1,0:T(8,128)} %get-tuple-element.64) | copy-start | bytes 9220
  195.7 12.8 %copy-start.77 = (f32[2,128]{1,0:T(2,128)}, f32[2,128]{1,0:T(2,128)S(1)}, u32[]{:S(2)}) copy-start(f32[2,128]{1,0:T(2,128)S(1)} %broadcast_multiply_fusion.1) | copy-start | bytes 3076
  195.7 6.2 %slice-start.2 = ((s8[4718592]{0:T(1024)(128)(4,1)}), s8[4194304]{0:T(1024)(128)(4,1)S(1)}, s32[]{:S(2)}) async-start(s8[4718592]{0:T(1024)(128)(4,1)} %bitcast.410), calls=%async_computation.2 | async-start | bytes 8388608
  197.8 10.7 %copy-start.81 = (f32[2,128]{1,0:T(2,128)}, f32[2,128]{1,0:T(2,128)S(1)}, u32[]{:S(2)}) copy-start(f32[2,128]{1,0:T(2,128)S(1)} %fusion.74) | copy-start | bytes 3076
  197.8 4.2 copy-start.26
  197.8 4.2 slice-start.3
  202.0 6.5 %slice-start = ((s8[4718592]{0:T(1024)(128)(4,1)}), s8[4194304]{0:T(1024)(128)(4,1)S(1)}, s32[]{:S(2)}) async-start(s8[4718592]{0:T(1024)(128)(4,1)} %bitcast.354), calls=%async_computation | async-start | bytes 8388608
  204.8 3.7 slice-start.1
  214.2 3.3 copy-start.55
  219.7 5.1 %copy-start.35 = (bf16[2,128,2304]{1,2,0:T(8,128)(2,1)S(1)}, bf16[2,128,2304]{1,2,0:T(8,128)(2,1)}, u32[]{:S(2)}) copy-start(bf16[2,128,2304]{1,2,0:T(8,128)(2,1)} %copy.101) | copy-start | bytes 3538948
  221.7 3.1 copy-start.25
  221.8 3.1 copy-start.41
  233.9 11.5 %copy-start.4 = (bf16[1,4,2,96,768]{4,3,2,1,0:T(8,128)(2,1)S(1)}, bf16[1,4,2,96,768]{4,3,2,1,0:T(8,128)(2,1)}, u32[]{:S(2)}) copy-start(bf16[1,4,2,96,768]{4,3,2,1,0:T(8,128)(2,1)} %copy-done.2) | copy-start | bytes 3538948
  247.0 10.5 %copy-start.28 = (f32[2,64,768]{2,1,0:T(8,128)S(1)}, f32[2,64,768]{2,1,0:T(8,128)}, u32[]{:S(2)}) copy-start(f32[2,64,768]{2,1,0:T(8,128)} %get-tuple-element.70) | copy-start | bytes 1179652
  247.0 10.5 %copy-start.84 = (f32[2,64]{1,0:T(2,128)S(1)}, f32[2,64]{1,0:T(2,128)}, u32[]{:S(2)}) copy-start(f32[2,64]{1,0:T(2,128)} %copy-done.83) | copy-start | bytes 1540
  247.0 11.8 %copy-start.98 = (f32[2,64]{1,0:T(2,128)S(1)}, f32[2,64]{1,0:T(2,128)}, u32[]{:S(2)}) copy-start(f32[2,64]{1,0:T(2,128)} %copy-done.97) | copy-start | bytes 1540
  247.0 11.8 %copy-start.92 = (f32[2,64]{1,0:T(2,128)S(1)}, f32[2,64]{1,0:T(2,128)}, u32[]{:S(2)}) copy-start(f32[2,64]{1,0:T(2,128)} %copy-done.91) | copy-start | bytes 1540
  248.3 11.8 %copy-start.100 = (f32[2,64]{1,0:T(2,128)S(1)}, f32[2,64]{1,0:T(2,128)}, u32[]{:S(2)}) copy-start(f32[2,64]{1,0:T(2,128)} %get-tuple-element.85) | copy-start | bytes 1540
  248.3 12.1 %copy-start.34 = (bf16[4,32,768]{2,1,0:T(8,128)(2,1)S(1)}, bf16[4,32,768]{2,1,0:T(8,128)(2,1)}, u32[]{:S(2)}) copy-start(bf16[4,32,768]{2,1,0:T(8,128)(2,1)} %slot_gather.1) | copy-start | bytes 589828
  248.4 12.3 %copy-start.7 = (bf16[1,2,96,768]{3,2,1,0:T(8,128)(2,1)S(1)}, bf16[1,2,96,768]{3,2,1,0:T(8,128)(2,1)}, u32[]{:S(2)}) copy-start(bf16[1,2,96,768]{3,2,1,0:T(8,128)(2,1)} %copy-done.5) | copy-start | bytes 884740
  257.5 3.4 copy-start.107
  257.5 3.4 copy-start.109
  257.5 3.4 copy-start.45
  261.4 12.3 %copy-start.23 = (f32[2,64,768]{2,1,0:T(8,128)S(1)}, f32[2,64,768]{2,1,0:T(8,128)}, u32[]{:S(2)}) copy-start(f32[2,64,768]{2,1,0:T(8,128)} %slot_sum.5) | copy-start | bytes 1179652
  261.4 12.3 %copy-start.86 = (f32[2,64]{1,0:T(2,128)S(1)}, f32[2,64]{1,0:T(2,128)}, u32[]{:S(2)}) copy-start(f32[2,64]{1,0:T(2,128)} %copy-done.85) | copy-start | bytes 1540
  262.5 12.4 %copy-start.96 = (f32[2,64]{1,0:T(2,128)S(1)}, f32[2,64]{1,0:T(2,128)}, u32[]{:S(2)}) copy-start(f32[2,64]{1,0:T(2,128)} %copy-done.95) | copy-start | bytes 1540
  263.5 13.0 %copy-start.46 = (f32[2,128,768]{2,1,0:T(8,128)S(1)}, f32[2,128,768]{2,1,0:T(8,128)}, u32[]{:S(2)}) copy-start(f32[2,128,768]{2,1,0:T(8,128)} %add_add_fusion.2) | copy-start | bytes 2359300
  264.7 11.8 %copy-start.110 = (bf16[1,8,96]{2,1,0:T(8,128)(2,1)S(1)}, bf16[1,8,96]{2,1,0:T(8,128)(2,1)}, u32[]{:S(2)}) copy-start(bf16[1,8,96]{2,1,0:T(8,128)(2,1)} %stack.48) | copy-start | bytes 4612
  264.7 11.8 %copy-start.111 = (bf16[1,8,96]{2,1,0:T(8,128)(2,1)S(1)}, bf16[1,8,96]{2,1,0:T(8,128)(2,1)}, u32[]{:S(2)}) copy-start(bf16[1,8,96]{2,1,0:T(8,128)(2,1)} %stack.47) | copy-start | bytes 4612
  264.7 11.9 %copy-start.88 = (s32[32,8]{0,1:T(8,128)S(1)}, s32[32,8]{0,1:T(8,128)}, u32[]{:S(2)}) copy-start(s32[32,8]{0,1:T(8,128)} %copy-done.87) | copy-start | bytes 3076
  304.7 3.0 copy-start.40
  304.7 3.0 copy-start.60
  304.7 4.5 copy-start.58
  309.3 3.7 copy-start.43
  309.3 3.7 copy-start.56
  313.0 4.5 copy-start.50
  323.6 125.3 %copy-start.32 = (bf16[8,32,768]{2,1,0:T(8,128)(2,1)S(1)}, bf16[8,32,768]{2,1,0:T(8,128)(2,1)}, u32[]{:S(2)}) copy-start(bf16[8,32,768]{2,1,0:T(8,128)(2,1)} %slice.87) | copy-start | bytes 1179652
  448.3 3.2 copy-start.69
  (71 other events, 120.6 us)

commit v2 on v1

--- a/solution.py
+++ b/solution.py
@@ -571,9 +571,6 @@
             t = i - YD
             if 0 <= t < n: self.yarr(t)
             yield
-        for t in range(n): self.finish(t)
-        yield
-        for t in range(n): self.drain(t)
 
 
 def gather_sems(plan, count):
@@ -612,13 +609,7 @@
     return chunks
 
 
-def gather_kernel(plan, nin, *refs):
-    ins = refs[:nin]
-    outs = refs[nin : 2 * nin]
-    bounce = refs[2 * nin : 3 * nin]
-    zs, zr, xs, xr, ys, yr, cs, cr, ls = refs[3 * nin :]
-    sems = NS(zs=zs, zr=zr, xs=xs, xr=xr, ys=ys, yr=yr, cs=cs, cr=cr, ls=ls)
-    g = Gather(gather_chunks(plan, ins, outs), sems)
+def gather_enter(g, peers=()):
     bar = pltpu.get_barrier_semaphore()
     for pred, dev in g.barrier_peers():
         def sig(dev=dev): pl.semaphore_signal(bar, inc=1, device_id=dev, device_id_type=MESH)
@@ -629,8 +620,9 @@
     def _(): pl.semaphore_wait(bar, 5)
     @pl.when(jnp.logical_not(inner))
     def _(): pl.semaphore_wait(bar, 4)
-    st = g.steps()
-    next(st)
+
+
+def gather_own(g, plan, ins, outs, bounce, sems):
     kinds = {p[0]: p[1] for p in plan}
     def inside(a):
         i = ins[a].at[:, :, g.c] if kinds[a] == SHARED else ins[a]
@@ -643,22 +635,38 @@
         else: o = o.at[:, g.x]
         return pltpu.make_async_copy(bounce[a], o, sems.ls.at[a])
     def each(fn):
-        for a in range(nin):
+        for a in range(len(ins)):
             if kinds[a] == SINGLE:
                 @pl.when(g.z == g.slot)
                 def _(): fn(a)
             else: fn(a)
-    each(lambda a: inside(a).start())
     def turn(a):
         inside(a).wait()
         outside(a).start()
-    each(turn)
+    return (lambda: each(lambda a: inside(a).start())), (lambda: each(turn)), (lambda: each(lambda a: outside(a).wait()))
+
+
+def gather_kernel(plan, nin, *refs):
+    ins = refs[:nin]
+    outs = refs[nin : 2 * nin]
+    bounce = refs[2 * nin : 3 * nin]
+    zs, zr, xs, xr, ys, yr, cs, cr, ls = refs[3 * nin :]
+    sems = NS(zs=zs, zr=zr, xs=xs, xr=xr, ys=ys, yr=yr, cs=cs, cr=cr, ls=ls)
+    g = Gather(gather_chunks(plan, ins, outs), sems)
+    gather_enter(g)
+    st = g.steps()
     next(st)
-    each(lambda a: outside(a).wait())
+    own_start, own_turn, own_wait = gather_own(g, plan, ins, outs, bounce, sems)
+    own_start()
+    own_turn()
+    next(st)
+    own_wait()
     for _ in st: pass
-
-
-def gather_all(arrs, kinds, plan, cid, name):
+    for t in range(len(plan)): g.finish(t)
+    for t in range(len(plan)): g.drain(t)
+
+
+def gather_shapes(arrs, kinds):
     outs = []
     bounce = []
     for a, k in zip(arrs, kinds):
@@ -668,6 +676,11 @@
         elif k == ZONLY: s = (a.shape[0], 4) + a.shape[1:]
         else: s = (a.shape[0], 2) + a.shape[1:]
         outs.append(jax.ShapeDtypeStruct(s, a.dtype))
+    return outs, bounce
+
+
+def gather_all(arrs, kinds, plan, cid, name):
+    outs, bounce = gather_shapes(arrs, kinds)
     hbm = pl.BlockSpec(memory_space=pl.ANY)
     return pl.pallas_call(
         functools.partial(gather_kernel, plan, len(arrs)),
@@ -981,6 +994,217 @@
     return out.reshape(4 * part.shape[0], part.shape[1])
 
 
+class SlotSum:
+    def __init__(self, g, part, rc, s1, ry, fin, rf, ss, rs):
+        self.g, self.part, self.rc, self.s1, self.ry, self.fin, self.rf, self.ss, self.rs = g, part, rc, s1, ry, fin, rf, ss, rs
+        self.cps = []
+
+    def go(self, src, dst, i, dev):
+        k = self.g.cp(src, dst, self.ss.at[i], self.rs.at[i], dev)
+        k.start()
+        self.cps.append(k)
+        return k
+
+    def run(self, value, out, idle=lambda: None):
+        g, c = self.g, self.g.c
+        rows = value.shape[0] // 2
+        self.part[...] = value.astype(BF).reshape(2, rows, value.shape[1])
+        b = self.go(self.part.at[1 - c], self.rc, 0, g.cdev)
+        b.wait_recv()
+        self.s1[...] = (self.part[c].astype(F32) + self.rc[...].astype(F32)).astype(BF)
+        d = self.go(self.s1, self.ry, 1, g.ydev)
+        idle()
+        d.wait_recv()
+        total = (self.s1[...].astype(F32) + self.ry[...].astype(F32)).astype(BF)
+        self.fin[...] = total
+        e = self.go(self.fin, self.rf, 2, g.cdev)
+        out[c] = total.astype(F32)
+        e.wait_recv()
+        out[1 - c] = self.rf[...].astype(F32)
+
+    def drain(self):
+        for k in self.cps:
+            k.wait_send()
+        self.cps = []
+
+
+def normed(v):
+    shifted = v - jnp.mean(v, axis=-1, keepdims=True)
+    scale = lax.rsqrt(jnp.mean(shifted * shifted, axis=-1, keepdims=True) + EPSILON)
+    return shifted * scale, scale
+
+
+def dot(a, b, ca=1, cb=0):
+    return lax.dot_general(a, b, (((ca,), (cb,)), ((), ())), preferred_element_type=F32)
+
+
+def gains_kernel_rows(parts):
+    rows = lax.broadcasted_iota(jnp.int32, (128, DIM), 0)
+    cols = lax.broadcasted_iota(jnp.int32, (128, DIM), 1)
+    total = None
+    for i in range(8):
+        sel = ((cols == rows + i * 96) & (rows < 96)).astype(BF)
+        t = dot(parts[i], sel)
+        total = t if total is None else total + t
+    return total
+
+
+def softmax_rows(scores, allowed):
+    scores = jnp.where(allowed, scores, MASKED)
+    e = jnp.exp(scores - jnp.max(scores, axis=-1, keepdims=True))
+    return e / jnp.sum(e, axis=-1, keepdims=True)
+
+
+def head_lanes(width, h):
+    lane = lax.broadcasted_iota(jnp.int32, (1, width), 1)
+    return (lane >= h * HEAD_DIM) & (lane < (h + 1) * HEAD_DIM)
+
+
+def forward_kernel(plan, nin, *refs):
+    ins = refs[:nin]
+    allow_ref = refs[nin]
+    outs = refs[nin + 1 : 2 * nin + 1]
+    start_o, joined_o, mixture_o, middle_o, expanded_o, patch_o, gains_o = refs[2 * nin + 1 : 2 * nin + 8]
+    rest = list(refs[2 * nin + 8 :])
+    bounce, rest = rest[:nin], rest[nin:]
+    (lookup_v, ids_v, gains_v, proj_v, wh_v, wm_v, wu_v, wd_v) = rest[:8]
+    (xp, rx, part, rc, s1, ry, fin, rf) = rest[8:16]
+    (xsem, ss, rs, vsem) = rest[16:20]
+    zs, zr, xs, xr, ys, yr, cs, cr, ls = rest[20:]
+    sems = NS(zs=zs, zr=zr, xs=xs, xr=xr, ys=ys, yr=yr, cs=cs, cr=cr, ls=ls)
+    g = Gather(gather_chunks(plan, ins, outs), sems)
+    gather_enter(g)
+    st = g.steps()
+    next(st)
+    own_start, own_turn, own_wait = gather_own(g, plan, ins, outs, bounce, sems)
+    own_start()
+    proj_v[...] = jnp.zeros_like(proj_v)
+    own_turn()
+    done = [0]
+
+    def pump(n=1):
+        for _ in range(n):
+            if done[0] < len(plan) + YD:
+                next(st)
+                done[0] += 1
+
+    pump()
+    own_wait()
+    where = {}
+    for t, p in enumerate(plan):
+        where.setdefault(p[0], []).append(t)
+
+    def until(a):
+        last = max(where[a])
+        kind = plan[last][1]
+        need = last + (2 * SP if kind == ZONLY else YD if kind == SHARED else XD) + 1
+        pump(max(0, need - done[0]))
+        if kind == SHARED:
+            for t in where[a]:
+                g.finish(t)
+
+    def take(src, dst, i):
+        k = pltpu.make_async_copy(src, dst, vsem.at[i])
+        k.start()
+        return k
+
+    E, I, GN, PJ, PH, PE, PR, PM = range(8)
+    until(I)
+    k1 = take(outs[I].at[0, g.z], ids_v, 0)
+    until(GN)
+    k2 = take(outs[GN].at[0], gains_v, 1)
+    until(PJ)
+    k3 = take(outs[PJ], proj_v.at[:, :, g.x], 2)
+    until(E)
+    k4 = [take(outs[E].at[:, :, 0, i // 2, i % 2], lookup_v.at[:, :, pl.ds(i * 8, 8), :], 3 + i) for i in range(4)]
+    for k in [k1, k2, k3] + k4:
+        k.wait()
+    gains = gains_kernel_rows(gains_v[...].reshape(8, 16, 128))
+    gains_o[...] = gains
+    lookup = lookup_v[...].reshape(256, DIM)
+    vocab_row = lax.broadcasted_iota(jnp.int32, (256, 128), 0)
+    proj = proj_v[...].reshape(2, DIM, DIM)
+    for xx in range(2):
+        total = None
+        for p in range(2):
+            hot = (vocab_row == ids_v[xx, pl.ds(g.slot * 2 + p, 1), :]).astype(BF)
+            tokens = dot(hot, lookup, 0, 0).astype(BF)
+            t = dot(tokens, proj[p])
+            total = t if total is None else total + t
+        xp[xx] = total.astype(BF)
+    kx = g.cp(xp.at[1 - g.x], rx, xsem.at[0], xsem.at[1], g.xdev)
+    kx.start()
+    until(PH)
+    k5 = take(outs[PH].at[0], wh_v, 0)
+    kx.wait_recv()
+    sums = [SlotSum(g, part.at[i], rc.at[i], s1.at[i], ry.at[i], fin.at[i], rf.at[i], ss.at[i], rs.at[i]) for i in range(3)]
+    sums[0].run(xp[g.x].astype(F32) + rx[...].astype(F32), start_o)
+    start = start_o[...].reshape(128, DIM)
+    norm_one = (normed(start)[0] * gains[0:1]).astype(BF)
+    k5.wait()
+    joined = dot(norm_one, wh_v[...].reshape(DIM, 576))
+    joined_o[...] = joined.astype(BF)
+    joined = joined.astype(BF).astype(F32)
+    q = joined[:, 0:192].astype(BF)
+    k = joined[:, 192:384].astype(BF)
+    v = joined[:, 384:576].astype(BF)
+    allowed = allow_ref[...] > 0
+    mixture = jnp.zeros((128, 192), F32)
+    for h in range(3):
+        lanes = head_lanes(192, h)
+        s = dot(jnp.where(lanes, q, jnp.zeros_like(q)), k, 1, 1) * HEAD_DIM ** (-0.5)
+        soft = softmax_rows(s, allowed).astype(BF)
+        mixture = jnp.where(lanes, dot(soft, v), mixture)
+    mixture = mixture.astype(BF)
+    mixture_o[...] = mixture
+    until(PM)
+    take(outs[PM].at[0], wm_v, 1).wait()
+    sums[1].run(dot(mixture, wm_v[...].reshape(192, DIM)), patch_o)
+    middle = start + patch_o[...].reshape(128, DIM)
+    middle_o[...] = middle
+    norm_two = (normed(middle)[0] * gains[1:2]).astype(BF)
+    until(PE)
+    take(outs[PE].at[0], wu_v, 0).wait()
+    expanded = dot(norm_two, wu_v[...].reshape(DIM, DIM))
+    expanded_o[...] = expanded
+    hidden = gelu_tanh(expanded).astype(BF)
+    until(PR)
+    take(outs[PR].at[0], wd_v, 1).wait()
+    sums[2].run(dot(hidden, wd_v[...].reshape(DIM, DIM)), patch_o)
+    patch_o[...] = patch_o[...] + middle.reshape(2, 64, DIM)
+    pump(len(plan) + YD)
+    for t in range(len(plan)):
+        if plan[t][0] != E:
+            g.finish(t)
+    for t in range(len(plan)):
+        g.drain(t)
+    kx.wait_send()
+    for s in sums:
+        s.drain()
+
+
+def forward_call(arrs, kinds, plan, allow):
+    outs, bounce = gather_shapes(arrs, kinds)
+    hbm = pl.BlockSpec(memory_space=pl.ANY)
+    vm = pl.BlockSpec(memory_space=pltpu.VMEM)
+    S = jax.ShapeDtypeStruct
+    V = lambda *s: pltpu.VMEM(s, BF)
+    D = pltpu.SemaphoreType.DMA
+    extra = [S((2, 64, DIM), F32), S((128, 576), BF), S((128, 192), BF), S((128, DIM), F32), S((128, DIM), F32), S((2, 64, DIM), F32), S((16, DIM), F32)]
+    scratch = [V(4, 2, 32, DIM), pltpu.VMEM((2, 8, 128), jnp.int32), V(4, 2, 16, 128), V(2, 4, 2, 96, DIM), V(4, 2, 96, 576), V(2, 96, DIM), V(4, 2, 96, DIM), V(4, 2, 96, DIM)]
+    scratch += [V(2, 128, DIM), V(128, DIM), V(3, 2, 64, DIM)] + [V(3, 64, DIM)] * 5
+    scratch += [D((2,)), D((3, 3)), D((3, 3)), D((7,))]
+    return pl.pallas_call(
+        functools.partial(forward_kernel, plan, len(arrs)),
+        out_shape=outs + extra,
+        in_specs=[hbm] * len(arrs) + [vm],
+        out_specs=[hbm] * len(outs) + [vm] * len(extra),
+        scratch_shapes=bounce + scratch + gather_sems(plan, len(arrs)),
+        compiler_params=pltpu.CompilerParams(collective_id=0, has_side_effects=True, vmem_limit_bytes=60 * 2**20),
+        name="gather_forward",
+    )(*arrs, allow)
+
+
 def mm(spec, a, b):
     return jnp.einsum(spec, a, b, preferred_element_type=F32)
 
@@ -1015,66 +1239,52 @@
     ff = patch_expand.shape[1]
     quarter = share // 4
     pick = lambda v, axis: lax.dynamic_index_in_dim(v, slot, axis, keepdims=False)
-    gains = jnp.concatenate([patch_prenorm, patch_midnorm, byte_prenorm, byte_midnorm])[None]
-    gains = jnp.pad(gains, ((0, share - vocab_part - 1), (0, width - 4 * share)))
-    misc = jnp.concatenate([embed_table, gains], axis=0)
+    gains = jnp.stack([patch_prenorm, patch_midnorm, byte_prenorm, byte_midnorm])
+    gains = jnp.pad(gains, ((0, 12), (0, 128 - share)))[None]
     heads_own = pick(patch_heads.reshape(share, 3, 4, width // 4), 2).reshape(1, share, 3 * width // 4)
     expand_own = pick(patch_expand.reshape(share, 8, 4, share), 2).reshape(1, share, width)
     reduce_own = pick(patch_reduce.reshape(4, share, width), 0)[None]
     shared = lambda v: v.reshape(v.shape[0] // share, 2, 2, quarter, v.shape[1])
     arrs = [
-        shared(misc), byte_ids.T[None], slot_project, heads_own, expand_own, reduce_own, patch_mixer[None],
+        embed_table.reshape(1, 2, 2, vocab_part // 4, width), byte_ids.T[None], gains, slot_project,
+        heads_own, expand_own, reduce_own, patch_mixer[None],
         shared(byte_heads), shared(byte_mixer), shared(byte_expand), shared(byte_reduce),
     ]
-    kinds = [SHARED, PRIVATE, ZONLY, PRIVATE, PRIVATE, PRIVATE, SINGLE] + [SHARED] * 4
-    plan = [(0, SHARED, 0, 0, width), (1, PRIVATE, 0, 0, 0)]
-    plan += [(7, SHARED, 0, i * width, width) for i in range(3)] + [(8, SHARED, 0, 0, width)]
-    plan += [(9, SHARED, 0, i * width, width) for i in range(4)] + [(10, SHARED, i, 0, width) for i in range(4)]
-    plan += [(3, PRIVATE, 0, 0, 0), (6, SINGLE, 0, 0, 0), (4, PRIVATE, 0, 0, 0), (5, PRIVATE, 0, 0, 0)]
-    plan += [(2, ZONLY, 0, 0, 0), (2, ZONLY, 1, 0, 0)]
-    full = gather_all(arrs, kinds, plan, 0, "gather_weights")
-    misc_all = full[0].reshape(8, share, width)
-    lookup = misc_all[:, :vocab_part].reshape(vocab, width)
-    gains_all = misc_all[:, vocab_part, : 4 * share].reshape(8, 4, share).transpose(1, 0, 2).reshape(4, width)
-    gains_all = gains_all.astype(F32)
-    ids_all = full[1].reshape(8, patch_len, group_rows)
-    project = full[2].reshape(2, 4 * share, width)
-    p_heads = full[3].reshape(width, 3 * width // 4)
-    p_expand = full[4].reshape(width, width)
-    p_reduce = full[5].reshape(width, width)
-    p_mixer = full[6].reshape(width // 4, width)
-    b_heads = full[7].reshape(width, 3 * width)
-    b_mixer = full[8].reshape(width, width)
-    b_expand = full[9].reshape(width, ff)
-    b_reduce = full[10].reshape(ff, width)
-    vocab_iota = jnp.arange(vocab, dtype=jnp.int32)
-    hot = lambda ids: (ids[..., None] == vocab_iota).astype(BF)
-
-    z_ids = lax.dynamic_slice_in_dim(ids_all, (dp // 2) * 2, 2, 0)
-    pair_ids = lax.dynamic_slice_in_dim(z_ids, slot * 2, 2, 1)
-    lookup_parts = lookup.reshape(vocab, 4, 2, share)
-    lookup_x = lax.dynamic_index_in_dim(lookup_parts, x, 2, keepdims=False).reshape(vocab, 4 * share)
-    pair_tokens = mm("xpgv,vf->xpgf", hot(pair_ids), lookup_x).astype(BF)
-    start_part = mm("xpgf,pfe->xge", pair_tokens, project).astype(BF)
-    start = slot_sum(start_part, 2, True)
-
+    kinds = [SHARED, PRIVATE, PRIVATE, ZONLY, PRIVATE, PRIVATE, PRIVATE, SINGLE] + [SHARED] * 4
+    wide = [(8, SHARED, 0, i * width, width) for i in range(3)] + [(9, SHARED, 0, 0, width)]
+    wide += [(10, SHARED, 0, i * width, width) for i in range(4)] + [(11, SHARED, i, 0, width) for i in range(4)]
+    plan = [(1, PRIVATE, 0, 0, 0), (2, PRIVATE, 0, 0, 0), (0, SHARED, 0, 0, width)] + wide[:2]
+    plan += [(3, ZONLY, 0, 0, 0), (3, ZONLY, 1, 0, 0), (4, PRIVATE, 0, 0, 0)] + wide[2:4] + [(7, SINGLE, 0, 0, 0)]
+    plan += wide[4:5] + [(5, PRIVATE, 0, 0, 0)] + wide[5:7] + [(6, PRIVATE, 0, 0, 0)] + wide[7:]
     segments = seg_ids[0]
     pos = jnp.arange(group_rows, dtype=jnp.int32)
     allowed_patch = ((pos[:, None] >= pos[None, :]) & (segments[:, None] == segments[None, :]))[None]
+    full = forward_call(arrs, kinds, plan, allowed_patch[0].astype(F32))
+    start, joined, mixture, middle, expanded, patch_out, gains_all = full[12:]
+    lookup = full[0].reshape(vocab, width)
+    ids_all = full[1].reshape(8, patch_len, group_rows)
+    p_heads = full[4].reshape(width, 3 * width // 4)
+    p_expand = full[5].reshape(width, width)
+    p_reduce = full[6].reshape(width, width)
+    p_mixer = full[7].reshape(width // 4, width)
+    b_heads = full[8].reshape(width, 3 * width)
+    b_mixer = full[9].reshape(width, width)
+    b_expand = full[10].reshape(width, ff)
+    b_reduce = full[11].reshape(ff, width)
+    vocab_iota = jnp.arange(vocab, dtype=jnp.int32)
+    hot = lambda ids: (ids[..., None] == vocab_iota).astype(BF)
+    patch_out = patch_out.reshape(group_rows, width)
+    start = start.reshape(group_rows, width)
     heads = 3 * width // 4
     head_count = width // 4 // HEAD_DIM
     norm_one, back_one = jax.vjp(norm_rows, start, gains_all[0])
     norm_one = norm_one.astype(BF)
-    joined = mm("nd,df->nf", norm_one, p_heads).astype(BF).reshape(1, group_rows, 3, head_count, HEAD_DIM)
-    mixture, logsum = attention(joined[:, :, 0], joined[:, :, 1], joined[:, :, 2], allowed_patch)
-    mixture = mixture.astype(BF).reshape(group_rows, width // 4)
-    middle = start + slot_sum(mm("nf,fd->nd", mixture, p_mixer).astype(BF), 3)
+    joined = joined.reshape(1, group_rows, 3, head_count, HEAD_DIM)
     norm_two, back_two = jax.vjp(norm_rows, middle, gains_all[1])
     norm_two = norm_two.astype(BF)
-    expanded = mm("nd,df->nf", norm_two, p_expand)
     hidden, back_gelu = jax.vjp(gelu_tanh, expanded)
     hidden = hidden.astype(BF)
-    patch_out = middle + slot_sum(mm("nf,fd->nd", hidden, p_reduce).astype(BF), 4)
+    logsum = attention(joined[:, :, 0], joined[:, :, 1], joined[:, :, 2], allowed_patch)[1]
 
     first_row = slot * own_rows
     own_out = lax.dynamic_slice_in_dim(patch_out, first_row, own_rows, 0)

time: 474 us -> 439 us (0.926)
  matrix products: 67.5 us -> 50.7 us
  other arithmetic: 43.4 us -> 30.5 us
  local copies, waits for them, and re-layouts: 57.6 us -> 46.1 us
  Pallas kernels: 294 us -> 302 us
    pallas_call x0 -> x1, Pallas kernels: none -> 134 us  [forward_call(): pl.pallas_call(functools.partial(forward_kernel, plan, len(arrs)), out_sh...]
    pallas_call x2 -> x1, Pallas kernels: 112 us -> 19.6 us  [gather_all(): pl.pallas_call(functools.partial(gather_kernel, plan, len(arrs)), out_sha...]
    pallas_call x5 -> x2, Pallas kernels: 52 us -> 18.2 us  [slot_sum(): pl.pallas_call(functools.partial(sum_kernel, with_x), out_shape=jax.Shape...]
    unnamed x239 -> x183, local copies, waits for them, and re-layouts: 19.9 us -> 10.1 us
    dot_general x19 -> x14, matrix products: 22.2 us -> 18.5 us  [mm(): return jnp.einsum(spec, a, b, preferred_element_type=F32)]
where the time goes in v2:
time: 439 us; the launch traced here: 431 us
  Pallas kernels  302 us (69%)
  matrix products  50.7 us (12%)
  local copies, waits for them, and re-layouts  46.1 us (11%)
  other arithmetic  30.5 us (7%)
    pallas_call x1, Pallas kernels, forward_call(): pl.pallas_call(functools.partial(forward_kernel, plan, len(arrs)), out_sh...  134 us
    pallas_call x1, Pallas kernels, reduce_all(): pl.pallas_call(functools.partial(reduce_kernel, plan, len(al)), out_shape...  123 us
    pallas_call x1, Pallas kernels, gather_all(): pl.pallas_call(functools.partial(gather_kernel, plan, len(arrs)), out_sha...  19.6 us
    dot_general x14, matrix products, mm(): return jnp.einsum(spec, a, b, preferred_element_type=F32)  18.5 us
    pallas_call x2, Pallas kernels, slot_sum(): pl.pallas_call(functools.partial(sum_kernel, with_x), out_shape=jax.Shape...  18.2 us
    unnamed x183, local copies, waits for them, and re-layouts  10.1 us

profile of v2, /device:TPU:5, one launch (start us, length us, event | category | flops | bytes accessed | tf_op | source)
XLA Modules:
  0.0 431.0 jit_solution(11342917920163557690)
XLA Ops:
  0.7 1.4 fusion.77.refs_2_
  2.1 1.6 reshape.792
  5.8 1.2 dynamic-slice_reduce_fusion
  9.3 133.9 %gather_forward.1 = (bf16[4,2,1,2,2,8,768]{6,5,4,3,2,1,0:T(8,128)(2,1)}, s32[1,4,2,8,128]{4,3,2,1,0:T(8,128)}, bf16[1,4,2,16,128]{4,3,2,1,0:T(8,128)(2,1)}, bf16...) custom-call(bf16[1,2,2,8,768]{4,3,2,1,0:T(8,128)(2,1)} %bitcast.367,, ...), custom_call_target="tpu_custom_call" | custom-call | tf_op jit(solution)/shard_map/gather_forward/pallas_call | solution.py:1197
  144.9 1.5 fusion.98
  146.4 1.5 slice_reduce_fusion
  152.6 1.2 fusion.99
  156.9 1.5 fusion.65
  158.5 2.7 fusion.14
  161.2 3.7 fusion.4
  164.9 2.9 multiply_reduce_fusion.4
  167.8 1.3 stack.68
  169.2 1.4 add.162
  171.3 1.6 fusion.95
  174.6 1.2 convolution_convert_fusion.5
  175.9 1.2 copy.111
  181.8 1.1 copy-done.84
  183.0 1.1 fusion.102
  186.9 1.3 stack.67
  188.9 1.9 add_add_fusion.2
  190.8 2.1 reduce_sum.239.p_ref
  192.9 6.7 %slot_gather.1 = bf16[4,32,768]{2,1,0:T(8,128)(2,1)} custom-call(bf16[32,768]{1,0:T(8,128)(2,1)} %reduce_sum.239.p_ref), custom_call_target="tpu_custom_call" | custom-call | tf_op jit(solution)/shard_map/slot_gather/pallas_call | solution.py:985
  199.6 1.9 fusion.103
  201.6 1.3 convolution_convert_fusion.8
  202.9 9.1 %slot_sum.2 = f32[2,64,768]{2,1,0:T(8,128)} custom-call(bf16[2,64,768]{2,1,0:T(8,128)(2,1)} %bitcast.364), custom_call_target="tpu_custom_call" | custom-call | tf_op jit(solution)/shard_map/slot_sum/pallas_call | solution.py:941
  212.4 1.9 multiply_reduce_fusion.10
  217.2 2.3 convolution_convert_fusion.9
  219.5 9.1 %slot_sum.3 = f32[2,64,768]{2,1,0:T(8,128)} custom-call(bf16[2,64,768]{2,1,0:T(8,128)(2,1)} %bitcast.351), custom_call_target="tpu_custom_call" | custom-call | tf_op jit(solution)/shard_map/slot_sum/pallas_call | solution.py:941
  228.7 1.2 multiply_reduce_fusion.8
  230.6 2.4 fusion.43
  233.6 1.4 mul.566
  234.9 1.3 mul.562
  237.6 1.4 reshape.833
  239.0 2.1 convolution_bitcast_fusion.2
  243.7 19.6 %gather_d_start.1 = bf16[4,2,1,2,2,32,768]{6,5,4,3,2,1,0:T(8,128)(2,1)S(1)} custom-call(bf16[1,2,2,32,768]{4,3,2,1,0:T(8,128)(2,1)S(1)} %bitcast.301), custom_call_target="tpu_custom_call" | custom-call | tf_op jit(solution)/shard_map/gather_d_start/pallas_call | solution.py:685
  264.0 2.0 fusion.10
  269.5 1.2 copy.126
  271.2 3.0 bitcast_convert_fusion.2
  274.2 1.5 bitcast_convert_fusion.3
  275.7 3.7 bitcast_convert_fusion.1
  279.4 4.5 %bitcast_convert_fusion = bf16[3072,768]{1,0:T(8,128)(2,1)} fusion(bf16[2,128,768]{2,1,0:T(8,128)(2,1)S(1)} %bitcast.341, f32[2,128,3072]{2,1,0:T(8,128)S(1)} %copy-done.18), kind=kOutput, calls=%fused_computation | convolution fusion | flops 1217396736 | bytes 8257536 | tf_op jit(solution)/shard_map/bnf,bnd->fd/dot_general | solution.py:110
  284.3 1.3 copy.131
  285.7 1.8 convolution_convert_fusion.2
  287.5 1.6 convolution_convert_fusion.1
  290.1 123.2 %reduce_grads.1 = (bf16[1,2,2,24,768]{4,3,2,1,0:T(8,128)(2,1)}, bf16[1,2,2,24,2304]{4,3,2,1,0:T(8,128)(2,1)}, bf16[1,2,2,24,768]{4,3,2,1,0:T(8,128)(2,1)}, bf16[...) custom-call(bf16[4,2,1,2,2,24,768]{6,5,4,3,2,1,0:T(8,128)(2,1)} %bit, ...), custom_call_target="tpu_custom_call" | custom-call | tf_op jit(solution)/shard_map/reduce_grads/pallas_call | solution.py:881
  418.6 1.7 reshape.843
  422.8 2.6 reshape.844
  428.3 1.2 bitcast_convert_fusion.5
  (282 shorter events, 50.4 us)
Async XLA Ops:
  0.6 7.3 %copy-start = (bf16[384,768]{1,0:T(8,128)(2,1)S(1)}, bf16[384,768]{1,0:T(8,128)(2,1)}, u32[]{:S(2)}) copy-start(bf16[384,768]{1,0:T(8,128)(2,1)} %param.26) | copy-start | bytes 1769476
  0.7 4.4 %copy-start.40 = (bf16[96,3072]{1,0:T(8,128)(2,1)S(1)}, bf16[96,3072]{1,0:T(8,128)(2,1)}, u32[]{:S(2)}) copy-start(bf16[96,3072]{1,0:T(8,128)(2,1)} %param.25) | copy-start | bytes 1769476
  4.0 4.6 %copy-start.79 = (s32[1,128]{1,0:T(1,128)S(1)}, s32[1,128]{1,0:T(1,128)}, u32[]{:S(2)}) copy-start(s32[1,128]{1,0:T(1,128)} %param.18) | copy-start | bytes 1540
  8.6 135.6 %copy-start.64 = (s32[128,8]{0,1:T(8,128)S(1)}, s32[128,8]{0,1:T(8,128)}, u32[]{:S(2)}) copy-start(s32[128,8]{0,1:T(8,128)} %param.17) | copy-start | bytes 12292
  144.8 4.9 %copy-start.83 = (bf16[4,2,1,2,2,24,2304]{6,5,4,3,2,1,0:T(8,128)(2,1)S(1)}, bf16[4,2,1,2,2,24,2304]{6,5,4,3,2,1,0:T(8,128)(2,1)}, u32[]{:S(2)}) copy-start(bf16[4,2,1,2,2,24,2304]{6,5,4,3,2,1,0:T(8,128)(2,1)} %get-tuple-element.44) | copy-start | bytes 10616836
  151.6 2.5 copy-start.10
  153.8 3.2 slice-start
  154.1 2.8 slice-start.1
  156.1 2.3 slice-start.2
  156.9 8.0 %copy-start.58 = (f32[2,128]{1,0:T(2,128)}, f32[2,128]{1,0:T(2,128)S(1)}, u32[]{:S(2)}) copy-start(f32[2,128]{1,0:T(2,128)S(1)} %fusion.82) | copy-start | bytes 3076
  158.5 2.7 copy-start.17
  158.5 2.7 copy-start.24
  164.9 2.9 copy-start.27
  171.3 3.4 copy-start.9
  180.5 2.4 copy-start.84
  184.8 4.1 copy-start.3
  184.8 4.1 copy-start.25
  190.8 10.7 %copy-start.44 = (f32[128,768]{1,0:T(8,128)S(1)}, f32[128,768]{1,0:T(8,128)}, u32[]{:S(2)}) copy-start(f32[128,768]{1,0:T(8,128)} %get-tuple-element.50) | copy-start | bytes 1179652
  190.8 10.7 %copy-start.85 = (bf16[1,4,2,96,768]{4,3,2,1,0:T(8,128)(2,1)S(1)}, bf16[1,4,2,96,768]{4,3,2,1,0:T(8,128)(2,1)}, u32[]{:S(2)}) copy-start(bf16[1,4,2,96,768]{4,3,2,1,0:T(8,128)(2,1)} %get-tuple-element.51) | copy-start | bytes 3538948
  201.6 10.5 %copy-start.4 = (f32[128,768]{1,0:T(8,128)S(1)}, f32[128,768]{1,0:T(8,128)}, u32[]{:S(2)}) copy-start(f32[128,768]{1,0:T(8,128)} %get-tuple-element.52) | copy-start | bytes 1179652
  201.6 10.8 %copy-start.60 = (f32[768]{0:T(1024)S(1)}, f32[768]{0:T(1024)}, u32[]{:S(2)}) copy-start(f32[768]{0:T(1024)} %get-tuple-element.78) | copy-start | bytes 9220
  202.9 11.6 %copy-start.7 = (bf16[4,32,768]{2,1,0:T(8,128)(2,1)S(1)}, bf16[4,32,768]{2,1,0:T(8,128)(2,1)}, u32[]{:S(2)}) copy-start(bf16[4,32,768]{2,1,0:T(8,128)(2,1)} %slot_gather.1) | copy-start | bytes 589828
  212.0 2.3 copy-start.14
  212.2 2.5 copy-start.74
  212.2 2.5 copy-start.48
  212.4 2.6 copy-start.80
  212.4 2.6 copy-start.51
  216.0 12.6 %copy-start.5 = (f32[2,64,768]{2,1,0:T(8,128)S(1)}, f32[2,64,768]{2,1,0:T(8,128)}, u32[]{:S(2)}) copy-start(f32[2,64,768]{2,1,0:T(8,128)} %get-tuple-element.56) | copy-start | bytes 1179652
  219.5 13.5 %copy-start.63 = (f32[768]{0:T(1024)S(1)}, f32[768]{0:T(1024)}, u32[]{:S(2)}) copy-start(f32[768]{0:T(1024)} %get-tuple-element.74) | copy-start | bytes 9220
  219.5 19.5 %copy-start.19 = (f32[2,128,768]{2,1,0:T(8,128)S(1)}, f32[2,128,768]{2,1,0:T(8,128)}, u32[]{:S(2)}) copy-start(f32[2,128,768]{2,1,0:T(8,128)} %add_add_fusion.2) | copy-start | bytes 2359300
  228.7 4.9 %copy-start.69 = (f32[2,64]{1,0:T(2,128)}, f32[2,64]{1,0:T(2,128)S(1)}, u32[]{:S(2)}) copy-start(f32[2,64]{1,0:T(2,128)S(1)} %broadcast_multiply_fusion.1) | copy-start | bytes 1540
  233.0 9.8 %copy-start.6 = (f32[2,64,768]{2,1,0:T(8,128)S(1)}, f32[2,64,768]{2,1,0:T(8,128)}, u32[]{:S(2)}) copy-start(f32[2,64,768]{2,1,0:T(8,128)} %slot_sum.3) | copy-start | bytes 1179652
  233.6 9.1 %copy-start.70 = (f32[2,64]{1,0:T(2,128)S(1)}, f32[2,64]{1,0:T(2,128)}, u32[]{:S(2)}) copy-start(f32[2,64]{1,0:T(2,128)} %copy-done.69) | copy-start | bytes 1540
  271.2 3.0 copy-start.16
  271.2 3.0 copy-start.30
  275.7 3.7 copy-start.18
  275.7 3.7 copy-start.26
  279.4 4.5 %copy-start.32 = (bf16[1,128,3,3,64]{1,4,3,2,0:T(8,128)(2,1)S(1)}, bf16[1,128,3,3,64]{1,4,3,2,0:T(8,128)(2,1)}, u32[]{:S(2)}) copy-start(bf16[1,128,3,3,64]{1,4,3,2,0:T(8,128)(2,1)} %copy-done.31) | copy-start | bytes 442372
  279.4 4.5 %copy-start.36 = (bf16[2,64,768]{2,1,0:T(8,128)(2,1)S(1)}, bf16[2,64,768]{2,1,0:T(8,128)(2,1)}, u32[]{:S(2)}) copy-start(bf16[2,64,768]{2,1,0:T(8,128)(2,1)} %get-tuple-element.85) | copy-start | bytes 589828
  290.1 124.9 %copy-start.23 = (bf16[4,2,1,2,2,8,768]{6,5,4,3,2,1,0:T(8,128)(2,1)S(1)}, bf16[4,2,1,2,2,8,768]{6,5,4,3,2,1,0:T(8,128)(2,1)}, u32[]{:S(2)}) copy-start(bf16[4,2,1,2,2,8,768]{6,5,4,3,2,1,0:T(8,128)(2,1)} %get-tuple-element.41) | copy-start | bytes 1179652
  413.3 2.5 copy-start.35
  414.3 3.2 copy-start.42
  418.6 2.4 copy-start.41
  422.8 2.7 copy-start.39
  425.4 2.1 copy-start.52
  425.4 2.9 copy-start.38
  426.6 2.9 copy-start.37
  428.3 2.3 copy-start.1
  (43 other events, 51.7 us)
